TPU v7x, 32 devices: a whole 2x2x4 slice. The times are simulated.
32 devices in a mesh: user: 4 (over x, core), item: 8 (over z, y).
Axes of the slice: x: 2, y: 2, z: 4, core: 2. Of those that a mesh axis runs over, the one named last changes fastest.
Arguments:
- item_feats: bfloat16 [131072, 1024], P(('user', 'item')), may hold values from -30 to 30
- first_weight: bfloat16 [1024, 512], replicated, may hold values from -0.1875 to 0.1875
- second_weight: bfloat16 [512, 256], replicated, may hold values from -0.25 to 0.25
- counts: int32 [131072], P(('user', 'item')), may hold values from 1 to 245760
- user_embed: bfloat16 [8192, 256], P(('user', 'item')), may hold values from -1 to 1
- list_owner: int32 [4096, 1], P(('user', 'item')), may hold values from 0 to 31, as said below
- list_slot: int32 [4096], P(('user', 'item')), may hold values from 0 to 31
- positive: int32 [8192], P(('user', 'item')), may hold values from 0 to 2047
Outputs:
- user_loss: float32 [8192], P(('user', 'item'))
- user_gradient: float32 [8192, 256], P(('user', 'item'))
- first_gradient: float32 [1024, 512], replicated
- second_gradient: float32 [512, 256], replicated
Inputs may be any that keep to these rules, and one draw needn't show every extreme that they name: `list_owner`: the rows of one device (128 of them, an aligned block) name any one owner at most 8 times; in every draw one owner is named exactly 8 times in the rows of every device.
All inputs are finite; a program needn't handle non-finite values.
Results may differ from a plain program's by a relative error of at most 0.0064.
Values may be sent and summed in bfloat16 or wider, within the bound.
No kernel may reach another device: no remote copies, remote signals or barrier semaphores. Data moves between devices by JAX's collectives and lax.ppermute only.
A program may use at most 192 MiB of HBM per device.

v0:
```python
import jax
import jax.numpy as jnp
from jax import lax
from jax.sharding import PartitionSpec as P

BLK = 128
NQ = 8
QB = 16


LOGIT_SCALE = 20.0
LOSS_SCALE = 4096.0
NORM_EPSILON = 1e-06


def body(
    item_feats, first_weight, second_weight, counts, user_embed, list_owner, list_slot, positive
):
    devices = lax.axis_size(("user", "item"))
    item_rows = item_feats.shape[0]
    own_blocks = item_rows // BLK
    user_rows = user_embed.shape[0]
    requests = list_slot.shape[0]
    capacity = 2 * requests // devices
    group_size = user_rows // NQ
    all_users = user_rows * devices
    linear_one = jnp.dot(item_feats, first_weight, preferred_element_type=jnp.float32)
    hidden = jnp.maximum(linear_one, 0.0).astype(jnp.bfloat16)
    tower_out = jnp.dot(hidden, second_weight, preferred_element_type=jnp.float32)
    item_norm = lax.rsqrt(jnp.sum(tower_out * tower_out, axis=1, keepdims=True) + NORM_EPSILON)
    vector_blocks = (tower_out * item_norm).astype(jnp.bfloat16).reshape(own_blocks, BLK, -1)
    log_blocks = jnp.log(counts.astype(jnp.float32)).astype(jnp.bfloat16).reshape(own_blocks, BLK)
    user_float = user_embed.astype(jnp.float32)
    user_norm = lax.rsqrt(jnp.sum(user_float * user_float, axis=1, keepdims=True) + NORM_EPSILON)
    user_vector = (user_float * user_norm).astype(jnp.bfloat16)
    group_users = user_vector.reshape(NQ, group_size, -1)
    group_pos = positive.reshape(NQ, group_size)
    owners = list_owner[:, 0]
    one_hot = (owners[:, None] == jnp.arange(devices, dtype=jnp.int32)[None, :]).astype(jnp.int32)
    earlier = jnp.cumsum(one_hot, axis=0) - one_hot
    position = owners * capacity + jnp.sum(earlier * one_hot, axis=1)
    send_slots = (
        jnp.zeros((devices * capacity,), jnp.int32)
        .at[position]
        .set(list_slot)
        .reshape(devices, capacity)
    )
    index_rows = jnp.arange(requests, dtype=jnp.int32)
    list_index = index_rows // QB
    offset = index_rows % QB * BLK
    local_pos = group_pos[list_index] - offset[:, None]
    local_pos = jnp.where((local_pos >= 0) & (local_pos < BLK), local_pos, -1)
    slot_users = (
        jnp.zeros((devices * capacity, group_size, group_users.shape[2]), jnp.bfloat16)
        .at[position]
        .set(group_users[list_index])
    )
    slot_pos = jnp.full((devices * capacity, group_size), -1, jnp.int32).at[position].set(local_pos)
    slot_ids, pos_in = (
        lax.all_to_all(send_slots, ("user", "item"), split_axis=0, concat_axis=0, tiled=True),
        lax.all_to_all(
            slot_pos.reshape(devices, capacity, group_size),
            ("user", "item"),
            split_axis=0,
            concat_axis=0,
            tiled=True,
        ),
    )
    users_in = lax.all_to_all(
        slot_users.reshape(devices, capacity, group_size, -1),
        ("user", "item"),
        split_axis=0,
        concat_axis=0,
        tiled=True,
    )
    blocks_in = vector_blocks[slot_ids]
    logs_in = log_blocks[slot_ids].astype(jnp.float32)
    scores = (
        LOGIT_SCALE
        * jnp.einsum("nkue,nkbe->nkub", users_in, blocks_in, preferred_element_type=jnp.float32)
        - logs_in[:, :, None, :]
    )
    exp_scores = jnp.exp(scores)
    is_positive = jnp.arange(BLK, dtype=jnp.int32)[None, None, None, :] == pos_in[:, :, :, None]
    part_totals = jnp.sum(exp_scores, axis=3)
    part_pos = jnp.sum(jnp.where(is_positive, scores, 0.0), axis=3)
    back_totals, back_pos = (
        lax.all_to_all(part_totals, ("user", "item"), split_axis=0, concat_axis=0, tiled=True),
        lax.all_to_all(part_pos, ("user", "item"), split_axis=0, concat_axis=0, tiled=True),
    )
    totals = (
        back_totals.reshape(devices * capacity, group_size)[position]
        .reshape(NQ, QB, group_size)
        .sum(axis=1)
    )
    pos_score = (
        back_pos.reshape(devices * capacity, group_size)[position]
        .reshape(NQ, QB, group_size)
        .sum(axis=1)
    )
    user_loss = jnp.log(totals) - pos_score
    slot_totals = (
        jnp.ones((devices * capacity, group_size), jnp.float32).at[position].set(totals[list_index])
    )
    totals_in = lax.all_to_all(
        slot_totals.reshape(devices, capacity, group_size),
        ("user", "item"),
        split_axis=0,
        concat_axis=0,
        tiled=True,
    )
    score_grad = (
        LOSS_SCALE
        / all_users
        * (exp_scores / totals_in[:, :, :, None] - is_positive.astype(jnp.float32))
    ).astype(jnp.bfloat16)
    returned = (
        LOGIT_SCALE
        * jnp.einsum("nkub,nkue->nkbe", score_grad, users_in, preferred_element_type=jnp.float32)
    ).astype(jnp.bfloat16)
    vector_parts = LOGIT_SCALE * jnp.einsum(
        "nkub,nkbe->nkue", score_grad, blocks_in, preferred_element_type=jnp.float32
    )
    parts_back = lax.all_to_all(
        vector_parts, ("user", "item"), split_axis=0, concat_axis=0, tiled=True
    )
    vector_grad = (
        parts_back.reshape(devices * capacity, group_size, -1)[position]
        .reshape(NQ, QB, group_size, -1)
        .sum(axis=1)
    )
    flat_ids = slot_ids.reshape(-1)
    selector = (jnp.arange(own_blocks, dtype=jnp.int32)[:, None] == flat_ids[None, :]).astype(
        jnp.bfloat16
    )
    item_gradient = jnp.dot(
        selector, returned.reshape(devices * capacity, -1), preferred_element_type=jnp.float32
    ).reshape(item_rows, -1)
    projection = jnp.sum(tower_out * item_gradient, axis=1, keepdims=True)
    out_gradient = (
        item_gradient * item_norm - tower_out * (projection * item_norm * item_norm * item_norm)
    ).astype(jnp.bfloat16)
    second_gradient = jnp.dot(hidden.T, out_gradient, preferred_element_type=jnp.float32)
    act_gradient = jnp.where(
        hidden > 0, jnp.dot(out_gradient, second_weight.T, preferred_element_type=jnp.float32), 0.0
    ).astype(jnp.bfloat16)
    first_gradient = jnp.dot(item_feats.T, act_gradient, preferred_element_type=jnp.float32)
    first_gradient, second_gradient = lax.psum((first_gradient, second_gradient), ("user", "item"))
    vector_grad = vector_grad.reshape(user_rows, -1)
    user_projection = jnp.sum(user_float * vector_grad, axis=1, keepdims=True)
    user_gradient = vector_grad * user_norm - user_float * (
        user_projection * user_norm * user_norm * user_norm
    )
    return (user_loss.reshape(user_rows), user_gradient, first_gradient, second_gradient)


def solution(mesh):
    return jax.shard_map(
        body,
        mesh=mesh,
        in_specs=(
            P(("user", "item"), None),
            P(),
            P(),
            P(("user", "item")),
            P(("user", "item"), None),
            P(("user", "item"), None),
            P(("user", "item")),
            P(("user", "item")),
        ),
        out_specs=(P(("user", "item")), P(("user", "item"), None), P(), P()),
        check_vma=False,
    )
```

profile of v0, /device:TPU:0, one launch (start us, length us, event | category | flops | bytes accessed | tf_op | source)
XLA Modules:
  0.0 490.5 jit_solution(11775205947933808178)
XLA Ops:
  7.2 0.8 fusion.13
  8.0 0.2 reduce_window_sum.11
  8.2 0.8 select_reduce_fusion.1
  9.0 0.7 fusion.27
  9.7 1.1 scatter_custom_fusion.1
  10.8 0.7 all_to_all.27
  11.5 7.3 %all-to-all-start.1 = ((s32[32,1,8]{2,1,0:T(1,128)}), s32[32,1,8]{2,1,0:T(1,128)S(1)}, u32[]{:S(2)}, u32[]{:S(2)}) async-start(s32[32,1,8]{2,1,0:T(1,128)} %bitcast.7), calls=%async_computation.1 | async-start | bytes 32768 | tf_op jit(solution)/shard_map/all_to_all | solution.py:60
  18.8 1.0 fusion.3
  19.9 0.8 reshape.192
  20.6 1.0 scatter_custom_fusion.2
  21.7 0.7 reshape.328
  22.4 3.4 all-to-all-done.1
  25.8 2.6 all-to-all-start.3
  28.4 1.0 fusion.4
  29.4 0.7 gather_fusion
  30.1 2.5 broadcast_in_dim.16
  32.6 15.7 %scatter_fusion = bf16[256,32,256]{2,1,0:T(8,128)(2,1)} fusion(bf16[256,32,256]{2,1,0:T(8,128)(2,1)} %broadcast_in_dim.16, s32[128]{0:T(128)S(1)} %fusion.27, bf16[128,32,256]{2,1,0:T(8,128)(2,1)S(1)} %gather_fusion), kind=kCustom, calls=%fused_computation.8 | custom fusion | bytes 6291968 | tf_op jit(solution)/shard_map/scatter | solution.py:56
  48.3 6.0 %all-to-all-start = ((bf16[32,8,32,256]{3,2,1,0:T(8,128)(2,1)}), bf16[32,8,32,256]{3,2,1,0:T(8,128)(2,1)}, u32[]{:S(2)}, u32[]{:S(2)}) async-start(bf16[32,8,32,256]{3,2,1,0:T(8,128)(2,1)} %bitcast.67), calls=%async_computation | async-start | bytes 8388608 | tf_op jit(solution)/shard_map/all_to_all | solution.py:69
  54.3 8.2 %maximum_convert_fusion = bf16[4096,512]{1,0:T(8,128)(2,1)S(1)} fusion(bf16[4096,1024]{1,0:T(8,128)(2,1)} %param.8, bf16[1024,512]{1,0:T(8,128)(2,1)S(1)} %copy-done), kind=kOutput, calls=%fused_computation.15 | convolution fusion | flops 4299161600 | bytes 13631488 | tf_op jit(solution)/shard_map/dot_general | solution.py:27
  62.5 1.3 multiply_reduce_fusion.1
  63.8 0.7 copy-done.5
  64.5 1.9 copy-done.2
  66.5 0.7 multiply_convert_fusion.2
  67.3 0.9 gather_fusion.2
  68.1 9.4 %gather_fusion.1 = bf16[256,128,256]{2,1,0:T(8,128)(2,1)} fusion(bf16[32,128,256]{2,1,0:T(8,128)(2,1)S(1)} %bitcast.62, s32[1024]{0:T(1024)S(1)} %pad_clamp_fusion.1), kind=kCustom, calls=%fused_computation.1 | custom fusion | bytes 33555456 | tf_op jit(solution)/shard_map/gather | solution.py:76
  77.6 0.5 broadcast.184
  78.1 0.7 reduce.4
  78.9 71.3 %all-to-all-done = bf16[32,8,32,256]{3,2,1,0:T(8,128)(2,1)} async-done(((bf16[32,8,32,256]{3,2,1,0:T(8,128)(2,1)}), bf16[32,8,32,256]{3,2,1,0:T(8,128)(2,1)}, u32[]{:S(2)}, u32[]{:S(2)}) %all-to-all-start) | async-done | bytes 4194336 | tf_op jit(solution)/shard_map/all_to_all | solution.py:69
  150.2 11.4 %exponential_reduce_fusion = (f32[32,8,32]{2,1,0:T(8,128)S(1)}, f32[32,8,32]{2,1,0:T(8,128)S(1)}, f32[32,8,32,128]{3,2,1,0:T(8,128)}) fusion(f32[32,8,128]{2,1,0:T(8,128)S(1)} %bitcast_convert_fusion, s32[32,8,32]{2,1,0:T(8,128)S(1)} %reshape.329, bf16[32,8,32,256]{3,2,1,0:T(8,128)(2,1)} %all-to-all-done, bf16[32,8,128,256]{3,2,1,0:T(8,128)(2,1)} %bitcast.63), kind=kOutput, calls=%fused_computation.26 | convolution fusion | flops 543145984 | bytes 25395200 | tf_op jit(solution)/shard_map/nkue,nkbe->nkub/dot_general | solution.py:80
  161.6 0.7 reshape.330
  162.3 2.6 all-to-all-start.4
  164.9 0.7 reshape.332
  165.6 6.5 %all-to-all-done.4 = f32[32,1,256]{2,1,0:T(1,128)S(1)} async-done(((f32[32,1,256]{2,1,0:T(1,128)}), f32[32,1,256]{2,1,0:T(1,128)S(1)}, u32[]{:S(2)}, u32[]{:S(2)}) %all-to-all-start.4) | async-done | bytes 32800 | tf_op jit(solution)/shard_map/all_to_all | solution.py:89
  172.1 2.7 all-to-all-start.2
  174.8 0.5 broadcast.185
  175.4 0.7 reduce.5
  176.2 5.8 %all-to-all-done.2 = f32[32,1,256]{2,1,0:T(1,128)S(1)} async-done(((f32[32,1,256]{2,1,0:T(1,128)}), f32[32,1,256]{2,1,0:T(1,128)S(1)}, u32[]{:S(2)}, u32[]{:S(2)}) %all-to-all-start.2) | async-done | bytes 32800 | tf_op jit(solution)/shard_map/all_to_all | solution.py:88
  182.0 0.7 reduce.6
  182.8 0.7 gather_fusion.4
  183.5 0.6 gather_fusion.3
  184.2 1.0 scatter_custom_fusion.3
  185.3 8.9 %all_to_all.42 = f32[32,1,256]{2,1,0:T(1,128)S(1)} all-to-all(f32[32,1,256]{2,1,0:T(1,128)S(1)} %reshape.334), channel_id=1, replica_groups=mesh['user'=4,'item'=8] {'user','item'}, dimensions={0} | all-to-all | bytes 65536 | tf_op jit(solution)/shard_map/all_to_all | solution.py:105
  194.2 0.7 reduce.7
  195.0 11.7 %broadcast_multiply_fusion = f32[32,8,32,256]{3,2,1,0:T(8,128)} fusion(bf16[32,8,128,256]{3,2,1,0:T(8,128)(2,1)} %bitcast.64, f32[32,8,32,128]{3,2,1,0:T(8,128)} %get-tuple-element.22, f32[32,8,32]{2,1,0:T(8,128)S(1)} %reshape.335, s32[32,8,32]{2,1,0:T(8,128)S(1)} %reshape.329, f32[32,8,128]{2,1,0:T(8,128)S(1)} %bitcast_convert_fusion), kind=kOutput, calls=%fused_computation.19 | convolution fusion | flops 547356672 | bytes 29556736 | tf_op jit(solution)/shard_map/nkub,nkbe->nkue/dot_general | solution.py:121
  206.7 3.7 all-to-all-start.6
  210.4 0.5 broadcast.183
  210.9 0.7 reduce.3
  211.7 13.0 %fusion = bf16[32,8,128,256]{3,2,1,0:T(8,128)(2,1)} fusion(bf16[32,8,32,256]{3,2,1,0:T(8,128)(2,1)} %all-to-all-done, f32[32,8,32,128]{3,2,1,0:T(8,128)} %get-tuple-element.22, f32[32,8,32]{2,1,0:T(8,128)S(1)} %reshape.335, s32[32,8,32]{2,1,0:T(8,128)S(1)} %reshape.329, f32[32,8,128]{2,1,0:T(8,128)S(1)} %bitcast_convert_fusion), kind=kOutput, calls=%fused_computation.13 | convolution fusion | flops 562036736 | bytes 25362432 | tf_op jit(solution)/shard_map/nkub,nkue->nkbe/dot_general | solution.py:119
  224.7 15.8 %copy.16 = bf16[32,8,128,256]{3,1,2,0:T(8,128)(2,1)S(1)} copy(bf16[32,8,128,256]{3,2,1,0:T(8,128)(2,1)} %fusion) | data formatting | bytes 33554432
  240.5 4.8 fusion.22
  245.3 4.9 reshape.201
  250.2 4.2 multiply_reduce_fusion
  254.4 0.4 copy-done.3
  254.8 1.3 copy-done.4
  256.1 2.4 subtract_convert_fusion
  258.5 2.1 fusion.33
  260.6 11.6 %fusion.2 = f32[1024,512]{0,1:T(8,128)} fusion(bf16[4096,1024]{1,0:T(8,128)(2,1)} %param.8, bf16[4096,512]{1,0:T(8,128)(2,1)} %copy-done.5, bf16[4096,256]{1,0:T(8,128)(2,1)S(1)} %subtract_convert_fusion, bf16[512,256]{1,0:T(8,128)(2,1)S(1)} %copy-done.9), kind=kOutput, calls=%fused_computation.28 | convolution fusion | flops 5375000576 | bytes 17039360 | tf_op jit(solution)/shard_map/dot_general | solution.py:147
  272.2 0.6 sub.52
  272.9 197.4 %all-reduce.3.cloned.1.call-done = (f32[1024,512]{0,1:T(8,128)}, f32[512,256]{1,0:T(8,128)}) async-done(((f32[1024,512]{0,1:T(8,128)}, f32[512,256]{1,0:T(8,128)}), (f32[1024,512]{0,1:T(8,128)}, f32[512,256]{1,0:T(8,128)})) %all-reduce.3.cloned.1.call-update) | async-done | bytes 2621456 | tf_op jit(solution)/shard_map/psum | solution.py:148
  470.2 2.9 copy.15
  473.1 6.2 %gather_fusion.5 = f32[128,32,256]{2,1,0:T(8,128)} fusion(f32[256,32,256]{2,1,0:T(8,128)} %bitcast.18, s32[1024]{0:T(1024)S(1)} %pad_clamp_fusion), kind=kCustom, calls=%fused_computation.7 | custom fusion | bytes 8389120 | tf_op jit(solution)/shard_map/gather | solution.py:128
  479.3 2.6 bitcast_reduce_fusion
  482.0 0.8 fusion.6
  482.9 0.8 copy.20
  (44 shorter events, 1.0 us)
Async XLA Ops:
  7.2 47.1 %copy-start = (bf16[1024,512]{1,0:T(8,128)(2,1)S(1)}, bf16[1024,512]{1,0:T(8,128)(2,1)}, u32[]{:S(2)}) copy-start(bf16[1024,512]{1,0:T(8,128)(2,1)} %param.9) | copy-start | bytes 3145732
  11.5 14.3 %all-to-all-start.1 = ((s32[32,1,8]{2,1,0:T(1,128)}), s32[32,1,8]{2,1,0:T(1,128)S(1)}, u32[]{:S(2)}, u32[]{:S(2)}) async-start(s32[32,1,8]{2,1,0:T(1,128)} %bitcast.7), calls=%async_computation.1 | async-start | bytes 32768 | tf_op jit(solution)/shard_map/all_to_all | solution.py:60
  25.8 22.4 %all-to-all-start.3 = ((s32[32,1,256]{2,1,0:T(1,128)}), s32[32,1,256]{2,1,0:T(1,128)S(1)}, u32[]{:S(2)}, u32[]{:S(2)}) async-start(s32[32,1,256]{2,1,0:T(1,128)} %reshape.328), calls=%async_computation.3 | async-start | bytes 65536 | tf_op jit(solution)/shard_map/all_to_all | solution.py:61
  48.3 6.0 %copy-start.10 = (s32[4096]{0:T(1024)S(1)}, s32[4096]{0:T(1024)}, u32[]{:S(2)}) copy-start(s32[4096]{0:T(1024)} %param.11) | copy-start | bytes 49156
  48.3 101.9 %all-to-all-start = ((bf16[32,8,32,256]{3,2,1,0:T(8,128)(2,1)}), bf16[32,8,32,256]{3,2,1,0:T(8,128)(2,1)}, u32[]{:S(2)}, u32[]{:S(2)}) async-start(bf16[32,8,32,256]{3,2,1,0:T(8,128)(2,1)} %bitcast.67), calls=%async_computation | async-start | bytes 8388608 | tf_op jit(solution)/shard_map/all_to_all | solution.py:69
  54.3 8.2 %copy-start.9 = (bf16[512,256]{1,0:T(8,128)(2,1)S(1)}, bf16[512,256]{1,0:T(8,128)(2,1)}, u32[]{:S(2)}) copy-start(bf16[512,256]{1,0:T(8,128)(2,1)} %param.10) | copy-start | bytes 786436
  62.5 2.0 copy-start.5
  64.5 1.9 copy-start.2
  162.3 9.8 %all-to-all-start.4 = ((f32[32,1,256]{2,1,0:T(1,128)}), f32[32,1,256]{2,1,0:T(1,128)S(1)}, u32[]{:S(2)}, u32[]{:S(2)}) async-start(f32[32,1,256]{2,1,0:T(1,128)} %reshape.330), calls=%async_computation.4 | async-start | bytes 65536 | tf_op jit(solution)/shard_map/all_to_all | solution.py:89
  172.1 9.9 %all-to-all-start.2 = ((f32[32,1,256]{2,1,0:T(1,128)}), f32[32,1,256]{2,1,0:T(1,128)S(1)}, u32[]{:S(2)}, u32[]{:S(2)}) async-start(f32[32,1,256]{2,1,0:T(1,128)} %reshape.332), calls=%async_computation.2 | async-start | bytes 65536 | tf_op jit(solution)/shard_map/all_to_all | solution.py:88
  206.7 266.4 %all-to-all-start.6 = ((f32[32,8,32,256]{3,2,1,0:T(8,128)}), f32[32,8,32,256]{3,2,1,0:T(8,128)}, u32[]{:S(2)}, u32[]{:S(2)}) async-start(f32[32,8,32,256]{3,2,1,0:T(8,128)} %broadcast_multiply_fusion), calls=%async_computation.6 | async-start | bytes 16777216 | tf_op jit(solution)/shard_map/all_to_all | solution.py:124
  210.4 259.9 %all-reduce.3.cloned.1.call-start = ((), (), s32[]{:S(2)}) async-start(), calls=%async_computation.7 | async-start | bytes 5242880 | tf_op jit(solution)/shard_map/psum | solution.py:148
  250.2 4.6 copy-start.3
  250.2 5.9 %copy-start.4 = (f32[4096,256]{1,0:T(8,128)S(1)}, f32[4096,256]{1,0:T(8,128)}, u32[]{:S(2)}) copy-start(f32[4096,256]{1,0:T(8,128)} %reshape.201) | copy-start | bytes 12582916
  256.1 2.4 copy-start.6
  473.1 10.6 %copy-start.1 = (bf16[1024,512]{1,0:T(8,128)(2,1)S(1)}, bf16[1024,512]{1,0:T(8,128)(2,1)}, u32[]{:S(2)}) copy-start(bf16[1024,512]{1,0:T(8,128)(2,1)} %param.9) | copy-start | bytes 3145732
  479.3 2.6 copy-start.7
  479.3 3.6 copy-start.8
Sparse Core Ops, SparseCore 0:
  272.3 197.8 all-reduce.2
where the time goes:
time: 492 us; the launch traced here: 491 us
  waiting for transfers between devices  284 us (58%)
  local copies, waits for them, and re-layouts  73.9 us (15%)
  matrix products  64 us (13%)
  starting transfers between devices  24.9 us (5%)
  other arithmetic  20.1 us (4%)
  between operations  14.4 us (3%)
  blocking collectives  8.88 us (2%)
    psum x1, waiting for transfers between devices, body(): lax.psum((first_gradient, second_gradient), ('user', 'item'))  197 us
    all_to_all x1, waiting for transfers between devices, body(): lax.all_to_all(slot_users.reshape(devices, capacity, group_size, -1), ('u...  71.3 us
    unnamed x33, local copies, waits for them, and re-layouts  26.5 us
    scatter x1, local copies, waits for them, and re-layouts, body(): slot_users = jnp.zeros((devices * capacity, group_size, group_users.shape...  15.7 us
    dot_general x1, matrix products, body(): jnp.einsum('nkub,nkue->nkbe', score_grad, users_in, preferred_element_typ...  13 us
    dot_general x1, matrix products, body(): jnp.einsum('nkub,nkbe->nkue', score_grad, blocks_in, preferred_element_ty...  11.7 us
    dot_general x1, matrix products, body(): jnp.dot(item_feats.T, act_gradient, preferred_element_type=jnp.float32)  11.6 us
    dot_general x1, matrix products, body(): jnp.einsum('nkue,nkbe->nkub', users_in, blocks_in, preferred_element_type...  11.4 us
  transfers between devices with their start and end apart: 7, of which 5 were waited for; matrix products, arithmetic and copies ran while one was open for 23% of the time, Pallas kernels for 0%

commit v1 on v0

v1 whole, which is shorter than its diff:
```python
import functools

import jax
import jax.numpy as jnp
import numpy as np
from jax import lax
from jax.experimental import pallas as pl
from jax.experimental.pallas import tpu as pltpu
from jax.sharding import PartitionSpec as P

BLK = 128
NQ = 8
QB = 16
SUB = 4

LOGIT_SCALE = 20.0
LOSS_SCALE = 4096.0
NORM_EPSILON = 1e-06

AXES = ("user", "item")
F32 = jnp.float32
BF16 = jnp.bfloat16
I32 = jnp.int32


class Links:
    def __init__(self):
        users = lax.axis_size("user")
        items = lax.axis_size("item")
        self.devices = users * items
        item_bits = items.bit_length() - 1
        user_bits = users.bit_length() - 1
        self.y = list(range(item_bits - 2))
        self.z = [item_bits - 1, item_bits - 2]
        self.core = item_bits
        self.x = list(range(item_bits + 1, item_bits + user_bits))

    def swap(self, value, mask):
        pairs = [(d, d ^ mask) for d in range(self.devices)]
        return lax.ppermute(value, AXES, pairs)


def join(parts):
    return parts[0] if len(parts) == 1 else jnp.concatenate(parts, axis=0)


def gather_plan(links):
    masks = [[0]]
    steps = []

    def add(bit, sources):
        steps.append((1 << bit, list(sources)))
        masks.append([m ^ (1 << bit) for s in sources for m in masks[s]])
        return len(masks) - 1

    base = [0]
    for bit in links.z:
        base.append(add(bit, base))
    first, second = base[:-1], base[-1:]
    for bit_a, bit_b in zip(links.y + links.x, links.x + links.y):
        new_a = add(bit_a, first)
        new_b = add(bit_b, second)
        first, second = first + [new_a], second + [new_b]
    return masks, steps


def scalar_copy(pieces, scratch, sems, per):
    offset = 0
    copies = []
    for index, piece in enumerate(pieces):
        rows = piece.shape[0]
        copies.append(
            pltpu.make_async_copy(piece, scratch.at[pl.ds(offset, rows), :], sems.at[index])
        )
        offset += rows
    return copies


def score_kernel(n_pieces, group, ul, tl, vq, cblk, nch, *refs):
    pieces = refs[:n_pieces]
    vectors, logs, loc, exp_out, totals_out, pos_out, users, t_acc, p_acc, sems = refs[n_pieces:]
    copies = scalar_copy(pieces, users, sems, group)
    for copy in copies:
        copy.start()
    t_acc[...] = jnp.zeros_like(t_acc)
    p_acc[...] = jnp.zeros_like(p_acc)
    for copy in copies:
        copy.wait()
    rows_iota = lax.broadcasted_iota(I32, (BLK, BLK), 0)
    lane_group = lax.broadcasted_iota(I32, (1, BLK), 1) // group

    def step(c, carry):
        first = pl.multiple_of(cblk[c] * BLK, BLK)
        block = vectors[pl.ds(first, BLK), :]
        members = jnp.concatenate(
            [users[pl.ds(pl.multiple_of(ul[c * SUB + i] * group, group), group), :] for i in range(SUB)],
            axis=0,
        )
        dots = lax.dot_general(block, members, (((1,), (1,)), ((), ())), preferred_element_type=F32)
        scores = LOGIT_SCALE * dots - logs[pl.ds(first, BLK), :]
        exp_scores = jnp.exp(scores)
        exp_out[pl.ds(pl.multiple_of(c * BLK, BLK), BLK), :] = exp_scores
        total = jnp.sum(exp_scores, axis=0, keepdims=True)
        is_positive = rows_iota == loc[pl.ds(c, 1), :]
        chosen = jnp.sum(jnp.where(is_positive, scores, 0.0), axis=0, keepdims=True)
        for i in range(SUB):
            keep = jnp.logical_and(lane_group == i, vq[c * SUB + i] > 0)
            row = tl[c * SUB + i]
            t_acc[pl.ds(row, 1), :] += jnp.where(keep, total, 0.0)
            p_acc[pl.ds(row, 1), :] += jnp.where(keep, chosen, 0.0)
        return carry

    lax.fori_loop(0, nch[0], step, 0)
    packed_rows = totals_out.shape[0]
    for acc, out in ((t_acc, totals_out), (p_acc, pos_out)):
        value = acc[...]
        both = value + pltpu.roll(value, 2 * group, axis=1)
        acc[...] = both + pltpu.roll(both, group, axis=1)
        packed = jnp.zeros((packed_rows, BLK), F32)
        for i in range(SUB):
            packed += jnp.where(lane_group == i, acc[pl.ds(i, packed_rows, stride=SUB), :], 0.0)
        out[...] = packed


def grad_kernel(
    n_pieces, group, scale, columns, with_items, ul, tl, vq, cblk, nch, *refs
):
    pieces = refs[:n_pieces]
    rest = refs[n_pieces:]
    vectors, exp_in, loc, totals = rest[:4]
    if with_items:
        keep_out, send_out, item_out, users, t_rep, v_acc, sems = rest[4:]
    else:
        keep_out, send_out, users, t_rep, v_acc, sems = rest[4:]
    copies = scalar_copy(pieces, users, sems, group)
    for copy in copies:
        copy.start()
    v_acc[...] = jnp.zeros_like(v_acc)
    if with_items:
        item_out[...] = jnp.zeros_like(item_out)
    rows_iota = lax.broadcasted_iota(I32, (BLK, BLK), 0)
    lane_group = lax.broadcasted_iota(I32, (1, BLK), 1) // group
    inverse = scale / totals[...]
    packed_rows = totals.shape[0]
    for i in range(SUB):
        part = jnp.where(lane_group == i, inverse, 0.0)
        part = part + pltpu.roll(part, 2 * group, axis=1)
        t_rep[pl.ds(i, packed_rows, stride=SUB), :] = part + pltpu.roll(part, group, axis=1)
    for copy in copies:
        copy.wait()
    low, high = columns

    def step(c, carry):
        first = pl.multiple_of(cblk[c] * BLK, BLK)
        weight = jnp.zeros((1, BLK), F32)
        for i in range(SUB):
            keep = jnp.logical_and(lane_group == i, vq[c * SUB + i] > 0)
            weight += jnp.where(keep, t_rep[pl.ds(tl[c * SUB + i], 1), :], 0.0)
        is_positive = rows_iota == loc[pl.ds(c, 1), :]
        exp_scores = exp_in[pl.ds(pl.multiple_of(c * BLK, BLK), BLK), :]
        grad = (exp_scores * weight - jnp.where(is_positive, scale, 0.0)).astype(BF16)
        starts = [pl.multiple_of(ul[c * SUB + i] * group, group) for i in range(SUB)]
        if with_items:
            members = jnp.concatenate([users[pl.ds(s, group), :] for s in starts], axis=0)
            item_out[pl.ds(first, BLK), :] += jnp.dot(grad, members, preferred_element_type=F32)
        block = vectors[pl.ds(first, BLK), low:high]
        parts = lax.dot_general(grad, block, (((0,), (0,)), ((), ())), preferred_element_type=F32)
        for i in range(SUB):
            v_acc[pl.ds(starts[i], group), :] += parts[i * group : (i + 1) * group]
        return carry

    lax.fori_loop(0, nch[0], step, 0)
    half = v_acc.shape[0] // 2
    keep_out[...] = (LOGIT_SCALE * v_acc[pl.ds(0, half), :]).astype(keep_out.dtype)
    send_out[...] = (LOGIT_SCALE * v_acc[pl.ds(half, half), :]).astype(BF16)


def any_spec():
    return pl.BlockSpec(memory_space=pl.ANY)


def vmem_spec():
    return pl.BlockSpec(memory_space=pltpu.VMEM)


def body(
    item_feats, first_weight, second_weight, counts, user_embed, list_owner, list_slot, positive
):
    links = Links()
    devices = links.devices
    me = lax.axis_index(AXES)
    item_rows, _ = item_feats.shape
    own_blocks = item_rows // BLK
    user_rows, emb = user_embed.shape
    requests = list_slot.shape[0]
    capacity = 2 * requests // devices
    group = user_rows // NQ
    all_users = user_rows * devices
    slots = devices * capacity
    lists = devices * NQ
    core = 1 << links.core

    user_float = user_embed.astype(F32)
    user_norm = lax.rsqrt(jnp.sum(user_float * user_float, axis=1, keepdims=True) + NORM_EPSILON)
    user_vector = (user_float * user_norm).astype(BF16)

    masks, steps = gather_plan(links)
    order = [m for piece in masks for m in piece]
    order = order + [m ^ core for m in order]
    place = np.zeros((devices,), np.int32)
    place[np.array(order)] = np.arange(devices, dtype=np.int32)

    pieces = [user_vector]
    for mask, sources in steps:
        pieces.append(links.swap(join([pieces[s] for s in sources]), mask))
    other = [links.swap(piece, core) for piece in pieces]
    all_pieces = pieces + other

    owners = list_owner[:, 0]
    same_owner = owners[:, None] == owners[None, :]
    request = jnp.arange(requests, dtype=I32)
    rank = jnp.sum((same_owner & (request[None, :] < request[:, None])).astype(I32), axis=1)
    position = owners * capacity + rank
    hit = position[:, None] == jnp.arange(slots, dtype=I32)[None, :]
    request_code = jnp.sum(jnp.where(hit, request[:, None] + 1, 0), axis=0)
    slot_code = jnp.sum(jnp.where(hit, list_slot[:, None], 0), axis=0)
    tables = jnp.concatenate([request_code, slot_code, positive])
    pad = -tables.shape[0] % (8 * BLK)
    tables = jnp.pad(tables, (0, pad)).reshape(1, -1, BLK)
    t_masks = [0]
    for bit in links.z + links.y + links.x + [links.core]:
        tables = jnp.concatenate([tables, links.swap(tables, 1 << bit)], axis=0)
        t_masks = t_masks + [m ^ (1 << bit) for m in t_masks]
    tables = tables.reshape(devices, -1)
    t_masks = np.array(t_masks)
    codes = lax.dynamic_slice(tables, (0, me * capacity), (devices, capacity)).reshape(-1)
    blocks = lax.dynamic_slice(tables, (0, slots + me * capacity), (devices, capacity)).reshape(-1)
    positions = tables[:, 2 * slots : 2 * slots + user_rows].reshape(lists, group)

    valid = codes > 0
    req = jnp.maximum(codes - 1, 0)
    in_list = req // QB
    kth = req % QB
    place_of = jnp.asarray(np.repeat(place[t_masks], capacity), I32)
    mask_of = jnp.asarray(np.repeat(t_masks, capacity), I32)
    source_of = jnp.asarray(np.repeat(np.arange(devices), capacity), I32)
    slot_index = jnp.arange(slots, dtype=I32)
    same_block = (blocks[:, None] == blocks[None, :]) & valid[None, :]
    block_rank = jnp.sum((same_block & (slot_index[None, :] < slot_index[:, None])).astype(I32), axis=1)
    block_index = jnp.arange(own_blocks, dtype=I32)
    one_hot = ((blocks[:, None] == block_index[None, :]) & valid[:, None]).astype(I32)
    chunks_of = (jnp.sum(one_hot, axis=0) + SUB - 1) // SUB
    start_of = jnp.sum(
        jnp.where(block_index[None, :] < block_index[:, None], chunks_of[None, :], 0), axis=1
    )
    n_chunks = jnp.sum(chunks_of).reshape(1)
    max_chunks = (slots + (SUB - 1) * own_blocks) // SUB
    spots = max_chunks * SUB
    spot_of = jnp.sum(one_hot * start_of[None, :], axis=1) * SUB + block_rank
    spot_of = jnp.where(valid, spot_of, -1)
    at_spot = spot_of[None, :] == jnp.arange(spots, dtype=I32)[:, None]

    def to_spot(value):
        return jnp.sum(jnp.where(at_spot, value[None, :], 0), axis=1)

    ul = to_spot(place_of * NQ + in_list)
    tl = to_spot((me ^ mask_of) * NQ + in_list)
    vq = to_spot(jnp.ones_like(codes))
    kq = to_spot(kth)
    jl = to_spot(source_of * NQ + in_list)
    chunk_index = jnp.arange(max_chunks, dtype=I32)
    cblk = (
        jnp.sum((start_of[None, :] <= chunk_index[:, None]).astype(I32), axis=1) - 1
    )
    local = positions[jl] - kq[:, None] * BLK
    local = jnp.where((local >= 0) & (local < BLK) & (vq[:, None] > 0), local, -1)
    local = local.reshape(max_chunks, SUB * group)

    linear_one = jnp.dot(item_feats, first_weight, preferred_element_type=F32)
    hidden = jnp.maximum(linear_one, 0.0).astype(BF16)
    tower_out = jnp.dot(hidden, second_weight, preferred_element_type=F32)
    item_norm = lax.rsqrt(jnp.sum(tower_out * tower_out, axis=1, keepdims=True) + NORM_EPSILON)
    vectors = (tower_out * item_norm).astype(BF16)
    logs = jnp.log(counts.astype(F32)).astype(BF16).astype(F32)
    logs = jnp.broadcast_to(logs[:, None], (item_rows, BLK))

    n_pieces = len(all_pieces)
    packed_rows = all_users // BLK
    limit = pltpu.CompilerParams(vmem_limit_bytes=60 * 1024 * 1024)
    exp_scores, part_totals, part_pos = pl.pallas_call(
        functools.partial(score_kernel, n_pieces, group),
        out_shape=(
            jax.ShapeDtypeStruct((max_chunks * BLK, BLK), F32),
            jax.ShapeDtypeStruct((packed_rows, BLK), F32),
            jax.ShapeDtypeStruct((packed_rows, BLK), F32),
        ),
        grid_spec=pltpu.PrefetchScalarGridSpec(
            num_scalar_prefetch=5,
            grid=(1,),
            in_specs=[any_spec()] * n_pieces + [vmem_spec()] * 3,
            out_specs=[vmem_spec()] * 3,
            scratch_shapes=[
                pltpu.VMEM((all_users, emb), BF16),
                pltpu.VMEM((lists, BLK), F32),
                pltpu.VMEM((lists, BLK), F32),
                pltpu.SemaphoreType.DMA((n_pieces,)),
            ],
        ),
        compiler_params=limit,
        name="scores",
    )(ul, tl, vq, cblk, n_chunks, *all_pieces, vectors, logs, local)

    sums = jnp.concatenate([part_totals, part_pos], axis=0)
    for bit in [links.core] + links.x + links.y + links.z[::-1]:
        sums = sums + links.swap(sums, 1 << bit)
    totals = sums[:packed_rows]
    own_rows = user_rows // BLK
    own_totals = lax.dynamic_slice(sums, (me * own_rows, 0), (own_rows, BLK))
    own_pos = lax.dynamic_slice(sums, (packed_rows + me * own_rows, 0), (own_rows, BLK))
    user_loss = (jnp.log(own_totals) - own_pos).reshape(user_rows)

    keep_type = F32 if all_users <= 8192 else BF16
    width = emb if all_users <= 8192 else BLK
    half_users = all_users // 2
    keeps, sends = [], []
    for low in range(0, emb, width):
        with_items = low == 0
        shapes = [
            jax.ShapeDtypeStruct((half_users, width), keep_type),
            jax.ShapeDtypeStruct((half_users, width), BF16),
        ]
        if with_items:
            shapes.append(jax.ShapeDtypeStruct((item_rows, emb), F32))
        outs = pl.pallas_call(
            functools.partial(
                grad_kernel, n_pieces, group, LOSS_SCALE / all_users, (low, low + width), with_items
            ),
            out_shape=shapes,
            grid_spec=pltpu.PrefetchScalarGridSpec(
                num_scalar_prefetch=5,
                grid=(1,),
                in_specs=[any_spec()] * n_pieces + [vmem_spec()] * 4,
                out_specs=[vmem_spec()] * len(shapes),
                scratch_shapes=[
                    pltpu.VMEM((all_users, emb), BF16),
                    pltpu.VMEM((lists, BLK), F32),
                    pltpu.VMEM((all_users, width), F32),
                    pltpu.SemaphoreType.DMA((n_pieces,)),
                ],
            ),
            compiler_params=limit,
            name="grads",
        )(ul, tl, vq, cblk, n_chunks, *all_pieces, vectors, exp_scores, local, totals)
        keeps.append(outs[0])
        sends.append(outs[1])
        if with_items:
            item_sum = outs[2]
    keep = keeps[0] if len(keeps) == 1 else jnp.concatenate(keeps, axis=1)
    send = sends[0] if len(sends) == 1 else jnp.concatenate(sends, axis=1)

    parts = keep.astype(F32) + links.swap(send, core).astype(F32)
    partial, offset = [], 0
    for piece in masks:
        rows = len(piece) * user_rows
        partial.append(parts[offset : offset + rows])
        offset += rows
    for index in range(len(steps) - 1, -1, -1):
        mask, sources = steps[index]
        arrived = links.swap(partial[index + 1].astype(BF16), mask).astype(F32)
        offset = 0
        for s in sources:
            rows = partial[s].shape[0]
            partial[s] = partial[s] + arrived[offset : offset + rows]
            offset += rows
    vector_grad = partial[0]
    user_projection = jnp.sum(user_float * vector_grad, axis=1, keepdims=True)
    user_gradient = vector_grad * user_norm - user_float * (
        user_projection * user_norm * user_norm * user_norm
    )

    item_gradient = LOGIT_SCALE * item_sum
    projection = jnp.sum(tower_out * item_gradient, axis=1, keepdims=True)
    out_gradient = (
        item_gradient * item_norm - tower_out * (projection * item_norm * item_norm * item_norm)
    ).astype(BF16)
    second_gradient = jnp.dot(hidden.T, out_gradient, preferred_element_type=F32)
    act_gradient = jnp.where(
        hidden > 0, jnp.dot(out_gradient, second_weight.T, preferred_element_type=F32), 0.0
    ).astype(BF16)
    first_gradient = jnp.dot(item_feats.T, act_gradient, preferred_element_type=F32)

    feat, hid = first_weight.shape
    fold = hid // emb
    tall = hid // fold
    packed = jnp.concatenate(
        [first_gradient]
        + [jnp.concatenate([second_gradient[i * tall : (i + 1) * tall] for i in range(fold)], axis=1)],
        axis=0,
    )
    total = sum_all(links, me, packed)
    first_total = total[:feat].astype(F32)
    second_total = jnp.concatenate(
        [total[feat:, i * emb : (i + 1) * emb] for i in range(fold)], axis=0
    ).astype(F32)
    return (user_loss, user_gradient, first_total, second_total)


def sum_all(links, me, value):
    rows = value.shape[0]
    half = rows // 2
    core_bit = (me >> links.core) & 1
    send = lax.dynamic_slice_in_dim(value, (1 - core_bit) * half, half, 0).astype(BF16)
    mine = lax.dynamic_slice_in_dim(value, core_bit * half, half, 0)
    mine = mine + links.swap(send, 1 << links.core).astype(F32)
    plane = links.x + links.y
    ways = 1 << len(plane)
    part = half // ways
    own = sum(((me >> bit) & 1) << i for i, bit in enumerate(plane))

    def mask_of(way):
        return sum(1 << bit for i, bit in enumerate(plane) if (way >> i) & 1)

    arrived = []
    for way in range(1, ways):
        out = lax.dynamic_slice_in_dim(mine, (own ^ way) * part, part, 0).astype(BF16)
        arrived.append(links.swap(out, mask_of(way)))
    own_sum = lax.dynamic_slice_in_dim(mine, own * part, part, 0)
    for item in arrived:
        own_sum = own_sum + item.astype(F32)
    for bit in links.z[::-1]:
        rounded = own_sum.astype(BF16)
        own_sum = rounded.astype(F32) + links.swap(rounded, 1 << bit).astype(F32)
    final = own_sum.astype(BF16)
    quarters = [final] + [links.swap(final, mask_of(way)) for way in range(1, ways)]
    for i in range(len(plane)):
        bit = (own >> i) & 1
        step = 1 << i
        quarters = [jnp.where(bit == 1, quarters[q ^ step], quarters[q]) for q in range(ways)]
    near = jnp.concatenate(quarters, axis=0)
    far = links.swap(near, 1 << links.core)
    return jnp.concatenate(
        [jnp.where(core_bit == 0, near, far), jnp.where(core_bit == 0, far, near)], axis=0
    )


def solution(mesh):
    return jax.shard_map(
        body,
        mesh=mesh,
        in_specs=(
            P(("user", "item"), None),
            P(),
            P(),
            P(("user", "item")),
            P(("user", "item"), None),
            P(("user", "item"), None),
            P(("user", "item")),
            P(("user", "item")),
        ),
        out_specs=(P(("user", "item")), P(("user", "item"), None), P(), P()),
        check_vma=False,
    )
```

time: 492 us -> 277 us (0.56)
  waiting for transfers between devices: 284 us -> 106 us
  local copies, waits for them, and re-layouts: 73.9 us -> 22.2 us
  matrix products: 64 us -> 24.3 us
  Pallas kernels: 0 us -> 37 us
  other arithmetic: 20.1 us -> 43.3 us
  starting transfers between devices: 24.9 us -> 41.9 us
  between operations: 14.4 us -> 1.47 us
  blocking collectives: 8.88 us -> 0 us
    psum x1 -> x0, waiting for transfers between devices: 197 us -> none  [body(): lax.psum((first_gradient, second_gradient), ('user', 'item'))]
    ppermute x0 -> x40, waiting for transfers between devices: none -> 106 us  [swap(): return lax.ppermute(value, AXES, pairs)]
    all_to_all x6 -> x0, waiting for transfers between devices: 87 us -> none  [the longest x1 71.3 us: body(): lax.all_to_all(slot_users.reshape(devices, capacity, group_size, -1), ('u...]
    ppermute x0 -> x40, starting transfers between devices: none -> 41.9 us  [swap(): return lax.ppermute(value, AXES, pairs)]
    dot_general x8 -> x4, matrix products: 64 us -> 24.3 us  [the longest x1 11.6 us: body(): jnp.dot(item_feats.T, act_gradient, preferred_element_type=F32)]
    pallas_call x0 -> x2, Pallas kernels: none -> 37 us  [the longest x1 20.5 us: body(): pl.pallas_call(functools.partial(grad_kernel, n_pieces, group, LOSS_SCALE...]
    all_to_all x6 -> x0, starting transfers between devices: 24.8 us -> none  [the longest x1 7.3 us: body(): lax.all_to_all(send_slots, ('user', 'item'), split_axis=0, concat_axis=0,...]
    unnamed x33 -> x77, local copies, waits for them, and re-layouts: 26.5 us -> 6.91 us
  transfers between devices with their start and end apart: 7 -> 40, of which waited for: 5 -> 25; matrix products, arithmetic and copies ran while one was open for 23% -> 20% of each run, Pallas kernels for 0% -> 0%
where the time goes in v1:
time: 277 us; the launch traced here: 276 us
  waiting for transfers between devices  106 us (38%)
  other arithmetic  43.3 us (16%)
  starting transfers between devices  41.9 us (15%)
  Pallas kernels  37 us (13%)
  matrix products  24.3 us (9%)
  local copies, waits for them, and re-layouts  22.2 us (8%)
    ppermute x40, waiting for transfers between devices, swap(): return lax.ppermute(value, AXES, pairs)  106 us
    ppermute x40, starting transfers between devices, swap(): return lax.ppermute(value, AXES, pairs)  41.9 us
    pallas_call x1, Pallas kernels, body(): pl.pallas_call(functools.partial(grad_kernel, n_pieces, group, LOSS_SCALE...  20.5 us
    pallas_call x1, Pallas kernels, body(): pl.pallas_call(functools.partial(score_kernel, n_pieces, group), out_shap...  16.5 us
    dot_general x1, matrix products, body(): jnp.dot(item_feats.T, act_gradient, preferred_element_type=F32)  11.6 us
    dot_general x1, matrix products, body(): linear_one = jnp.dot(item_feats, first_weight, preferred_element_type=F32)  8.1 us
    unnamed x77, local copies, waits for them, and re-layouts  6.91 us
    convert_element_type x7, other arithmetic, body(): arrived = links.swap(partial[index + 1].astype(BF16), mask).astype(F32)  6.69 us
  transfers between devices with their start and end apart: 40, of which 25 were waited for; matrix products, arithmetic and copies ran while one was open for 20% of the time, Pallas kernels for 0%

profile of v1, /device:TPU:0, one launch (start us, length us, event | category | flops | bytes accessed | tf_op | source)
XLA Modules:
  0.0 276.0 jit_solution(2454939054982920389)
XLA Ops:
  0.6 1.1 fusion.7
  2.8 4.1 %collective-permute-start.5 = (bf16[256,256]{1,0:T(8,128)(2,1)S(1)}, bf16[256,256]{1,0:T(8,128)(2,1)S(1)}, u32[]{:S(2)}, u32[]{:S(2)}) collective-permute-start(bf16[256,256]{1,0:T(8,128)(2,1)S(1)} %fusion.8.refs_0_), channel_id=1, source_target_pairs={{0,4},{1,5},{2,6},{3,7},{4,0},{5,1},{6,2},{7,3},{8,12},{9,13},{10,... | collective-permute-start | bytes 393224 | tf_op jit(solution)/shard_map/ppermute | solution.py:40
  10.2 8.1 %maximum_convert_fusion = bf16[4096,512]{1,0:T(8,128)(2,1)S(1)} fusion(bf16[4096,1024]{1,0:T(8,128)(2,1)} %param.11, bf16[1024,512]{1,0:T(8,128)(2,1)S(1)} %copy-done), kind=kOutput, calls=%fused_computation.2 | convolution fusion | flops 4299161600 | bytes 13631488 | tf_op jit(solution)/shard_map/dot_general | solution.py:279
  18.3 3.3 %multiply_reduce_fusion.1 = (f32[4096]{0:T(1024)S(1)}, f32[4096,256]{0,1:T(8,128)}) fusion(bf16[4096,512]{1,0:T(8,128)(2,1)S(1)} %maximum_convert_fusion, bf16[512,256]{1,0:T(8,128)(2,1)S(1)} %copy-done.22), kind=kOutput, calls=%fused_computation.7 | convolution fusion | flops 1075834880 | bytes 8667136 | tf_op jit(solution)/shard_map/dot_general | solution.py:281
  21.6 5.6 %copy.29 = f32[4096,256]{1,0:T(8,128)} copy(f32[4096,256]{0,1:T(8,128)} %get-tuple-element.73) | data formatting | bytes 8388608 | tf_op jit(solution)/shard_map/dot_general | solution.py:281
  27.2 3.6 %multiply_convert_fusion.refs_14_ = bf16[4096,256]{1,0:T(8,128)(2,1)} fusion(f32[4096,256]{1,0:T(8,128)} %copy.29, f32[4096]{0:T(1024)S(1)} %add_rsqrt_fusion), kind=kLoop, calls=%fused_computation.6 | loop fusion | flops 2097152 | bytes 6307840 | tf_op jit(solution)/shard_map/convert_element_type | solution.py:283
  30.8 1.9 collective-permute-start.1
  32.7 1.8 collective-permute-done.1
  34.5 1.8 collective-permute-start.2
  36.3 2.0 collective-permute-done.2
  38.3 1.7 collective-permute-start.3
  40.0 2.2 collective-permute-done.3
  45.3 1.9 collective-permute-start.6
  47.3 1.6 collective-permute-start.7
  48.8 5.0 %collective-permute-done.6.refs_2_ = bf16[512,256]{1,0:T(8,128)(2,1)S(1)} collective-permute-done((bf16[512,256]{1,0:T(8,128)(2,1)S(1)}, bf16[512,256]{1,0:T(8,128)(2,1)S(1)}, u32[]{:S(2)}, u32[]{:S(2)}) %collective-permute-start.6) | collective-permute-done | bytes 262176 | tf_op jit(solution)/shard_map/ppermute | solution.py:40
  53.8 1.7 collective-permute-start.8
  57.0 6.1 %collective-permute-done.8.refs_4_ = bf16[512,256]{1,0:T(8,128)(2,1)S(1)} collective-permute-done((bf16[512,256]{1,0:T(8,128)(2,1)S(1)}, bf16[512,256]{1,0:T(8,128)(2,1)S(1)}, u32[]{:S(2)}, u32[]{:S(2)}) %collective-permute-start.8) | collective-permute-done | bytes 262176 | tf_op jit(solution)/shard_map/ppermute | solution.py:40
  63.1 1.7 collective-permute-start.10
  66.0 6.7 %collective-permute-done.9.refs_5_ = bf16[1024,256]{1,0:T(8,128)(2,1)S(1)} collective-permute-done((bf16[1024,256]{1,0:T(8,128)(2,1)S(1)}, bf16[1024,256]{1,0:T(8,128)(2,1)S(1)}, u32[]{:S(2)}, u32[]{:S(2)}) %collective-permute-start.9) | collective-permute-done | bytes 524320 | tf_op jit(solution)/shard_map/ppermute | solution.py:40
  72.7 1.2 collective-permute-done.10.refs_6_
  76.6 1.6 gather_fusion
  80.8 2.7 broadcast_in_dim.125.refs_15_
  83.6 16.5 %scores.1 = (f32[11264,128]{1,0:T(8,128)}, f32[64,128]{1,0:T(8,128)}, f32[64,128]{1,0:T(8,128)}) custom-call(s32[352]{0:T(512)} %get-tuple-element.32.ul, s32[352]{0:T(512)} %get-tuple-element.31.tl, s32[352]{0:T(512)} %copy-done.24, s32[88]{0:T(128)} %broadcast_add_fusion.cblk, s32[1]{0:T(128)} %bitcast.6.nch, bf16[256,256]{1,0:T(8,128)(2,1)} %copy-done.8, ...), custom_call_target="tpu_custom_call" | custom-call | tf_op jit(solution)/shard_map/scores/pallas_call | solution.py:290
  101.6 7.2 %collective-permute-start.18 = (f32[128,128]{1,0:T(8,128)S(1)}, f32[128,128]{1,0:T(8,128)S(1)}, u32[]{:S(2)}, u32[]{:S(2)}) collective-permute-start(f32[128,128]{1,0:T(8,128)S(1)} %constant_dynamic-update-slice_fusion.5), channel_id=1, source_target_pairs={{0,8},{1,9},{2,10},{3,11},{4,12},{5,13},{6,14},{7,15},{8,0},{9,1},... | collective-permute-start | bytes 196616 | tf_op jit(solution)/shard_map/ppermute | solution.py:40
  109.8 4.3 %collective-permute-done.19 = f32[128,128]{1,0:T(8,128)S(1)} collective-permute-done((f32[128,128]{1,0:T(8,128)S(1)}, f32[128,128]{1,0:T(8,128)S(1)}, u32[]{:S(2)}, u32[]{:S(2)}) %collective-permute-start.19) | collective-permute-done | bytes 65568 | tf_op jit(solution)/shard_map/ppermute | solution.py:40
  114.2 4.3 %collective-permute-done.20 = f32[128,128]{1,0:T(8,128)S(1)} collective-permute-done((f32[128,128]{1,0:T(8,128)S(1)}, f32[128,128]{1,0:T(8,128)S(1)}, u32[]{:S(2)}, u32[]{:S(2)}) %collective-permute-start.20) | collective-permute-done | bytes 65568 | tf_op jit(solution)/shard_map/ppermute | solution.py:40
  118.6 4.3 %collective-permute-done.21 = f32[128,128]{1,0:T(8,128)S(1)} collective-permute-done((f32[128,128]{1,0:T(8,128)S(1)}, f32[128,128]{1,0:T(8,128)S(1)}, u32[]{:S(2)}, u32[]{:S(2)}) %collective-permute-start.21) | collective-permute-done | bytes 65568 | tf_op jit(solution)/shard_map/ppermute | solution.py:40
  122.9 5.3 %collective-permute-done.22 = f32[128,128]{1,0:T(8,128)S(1)} collective-permute-done((f32[128,128]{1,0:T(8,128)S(1)}, f32[128,128]{1,0:T(8,128)S(1)}, u32[]{:S(2)}, u32[]{:S(2)}) %collective-permute-start.22) | collective-permute-done | bytes 65568 | tf_op jit(solution)/shard_map/ppermute | solution.py:40
  128.8 20.5 %grads.1 = (f32[4096,256]{1,0:T(8,128)}, bf16[4096,256]{1,0:T(8,128)(2,1)}, f32[4096,256]{1,0:T(8,128)}) custom-call(s32[352]{0:T(512)} %get-tuple-element.32.ul, s32[352]{0:T(512)} %get-tuple-element.31.tl, s32[352]{0:T(512)} %copy-done.24, s32[88]{0:T(128)} %broadcast_add_fusion.cblk, s32[1]{0:T(128)} %bitcast.6.nch, bf16[256,256]{1,0:T(8,128)(2,1)} %copy-done.8, ...), custom_call_target="tpu_custom_call" | custom-call | tf_op jit(solution)/shard_map/grads/pallas_call | solution.py:334
  149.3 4.2 %multiply_reduce_fusion = f32[4096]{0:T(1024)S(1)} fusion(f32[4096,256]{1,0:T(8,128)} %copy.29, f32[4096,256]{1,0:T(8,128)} %get-tuple-element.15), kind=kLoop, calls=%fused_computation.4 | loop fusion | flops 3141632 | bytes 8404992 | tf_op jit(solution)/shard_map/reduce_sum | solution.py:382
  153.9 1.3 copy-done.3
  155.2 2.2 subtract_convert_fusion
  157.4 1.3 fusion.33
  158.7 11.6 %fusion.1 = f32[1024,512]{0,1:T(8,128)} fusion(bf16[4096,1024]{1,0:T(8,128)(2,1)} %param.11, bf16[4096,512]{1,0:T(8,128)(2,1)} %copy-done.4, bf16[4096,256]{1,0:T(8,128)(2,1)S(1)} %subtract_convert_fusion, bf16[512,256]{1,0:T(8,128)(2,1)S(1)} %copy-done.23), kind=kOutput, calls=%fused_computation.10 | convolution fusion | flops 5375000576 | bytes 17039360 | tf_op jit(solution)/shard_map/dot_general | solution.py:390
  170.4 1.8 maximum_maximum_fusion
  172.2 1.5 copy-done.6
  173.7 4.0 %collective-permute-start.30 = (bf16[640,512]{0,1:T(8,128)(2,1)S(1)}, bf16[640,512]{0,1:T(8,128)(2,1)S(1)}, u32[]{:S(2)}, u32[]{:S(2)}) collective-permute-start(bf16[640,512]{0,1:T(8,128)(2,1)S(1)} %dynamic-slice_convert_fusion), channel_id=1, source_target_pairs={{0,8},{1,9},{2,10},{3,11},{4,12},{5,13},{6,14},{7,15},{8,0},{9,1},... | collective-permute-start | bytes 1966088 | tf_op jit(solution)/shard_map/ppermute | solution.py:40
  177.9 1.8 collective-permute-done.30
  179.6 1.4 convert_add_fusion.1
  181.6 3.4 %collective-permute-start.31 = (bf16[160,512]{0,1:T(8,128)(2,1)S(1)}, bf16[160,512]{0,1:T(8,128)(2,1)S(1)}, u32[]{:S(2)}, u32[]{:S(2)}) collective-permute-start(bf16[160,512]{0,1:T(8,128)(2,1)S(1)} %get-tuple-element.49), channel_id=1, source_target_pairs={{0,16},{1,17},{2,18},{3,19},{4,20},{5,21},{6,22},{7,23},{8,24},{9,... | collective-permute-start | bytes 491528 | tf_op jit(solution)/shard_map/ppermute | solution.py:40
  185.0 6.6 %collective-permute-done.33 = bf16[160,512]{0,1:T(8,128)(2,1)S(1)} collective-permute-done((bf16[160,512]{0,1:T(8,128)(2,1)S(1)}, bf16[160,512]{0,1:T(8,128)(2,1)S(1)}, u32[]{:S(2)}, u32[]{:S(2)}) %collective-permute-start.33) | collective-permute-done | bytes 163872 | tf_op jit(solution)/shard_map/ppermute | solution.py:40
  191.6 4.2 %collective-permute-done.32 = bf16[160,512]{0,1:T(8,128)(2,1)S(1)} collective-permute-done((bf16[160,512]{0,1:T(8,128)(2,1)S(1)}, bf16[160,512]{0,1:T(8,128)(2,1)S(1)}, u32[]{:S(2)}, u32[]{:S(2)}) %collective-permute-start.32) | collective-permute-done | bytes 163872 | tf_op jit(solution)/shard_map/ppermute | solution.py:40
  196.0 7.8 %collective-permute-done.34 = bf16[160,512]{0,1:T(8,128)(2,1)S(1)} collective-permute-done((bf16[160,512]{0,1:T(8,128)(2,1)S(1)}, bf16[160,512]{0,1:T(8,128)(2,1)S(1)}, u32[]{:S(2)}, u32[]{:S(2)}) %collective-permute-start.34) | collective-permute-done | bytes 163872 | tf_op jit(solution)/shard_map/ppermute | solution.py:40
  203.9 13.4 %collective-permute-done.35 = bf16[160,512]{0,1:T(8,128)(2,1)S(1)} collective-permute-done((bf16[160,512]{0,1:T(8,128)(2,1)S(1)}, bf16[160,512]{0,1:T(8,128)(2,1)S(1)}, u32[]{:S(2)}, u32[]{:S(2)}) %collective-permute-start.35) | collective-permute-done | bytes 163872 | tf_op jit(solution)/shard_map/ppermute | solution.py:40
  217.4 2.2 collective-permute-start.36
  219.7 1.3 collective-permute-start.38
  220.9 5.4 %fusion.27 = (bf16[4096,256]{1,0:T(8,128)(2,1)S(1)}, f32[4096,256]{1,0:T(8,128)}) fusion(f32[4096,256]{1,0:T(8,128)} %get-tuple-element.13, bf16[4096,256]{1,0:T(8,128)(2,1)} %collective-permute-done.23), kind=kLoop, calls=%fused_computation.137 | loop fusion | flops 3145728 | bytes 12582912 | tf_op jit(solution)/shard_map/convert.1
  226.4 1.5 collective-permute-start.26
  227.9 1.2 collective-permute-start.24
  229.1 3.1 %collective-permute-done.37 = bf16[160,512]{0,1:T(8,128)(2,1)S(1)} collective-permute-done((bf16[160,512]{0,1:T(8,128)(2,1)S(1)}, bf16[160,512]{0,1:T(8,128)(2,1)S(1)}, u32[]{:S(2)}, u32[]{:S(2)}) %collective-permute-start.37) | collective-permute-done | bytes 163872 | tf_op jit(solution)/shard_map/ppermute | solution.py:40
  233.2 1.0 broadcast_select_fusion.9
  234.3 1.3 pad_maximum_fusion.1
  235.6 7.8 %collective-permute-done.26 = bf16[1024,256]{1,0:T(8,128)(2,1)S(1)} collective-permute-done((bf16[1024,256]{1,0:T(8,128)(2,1)S(1)}, bf16[1024,256]{1,0:T(8,128)(2,1)S(1)}, u32[]{:S(2)}, u32[]{:S(2)}) %collective-permute-start.26) | collective-permute-done | bytes 524320 | tf_op jit(solution)/shard_map/ppermute | solution.py:40
  243.5 1.1 convert_element_type.137
  244.6 2.4 fusion.6
  247.0 1.2 collective-permute-start.27
  249.9 5.6 %collective-permute-done.27 = bf16[512,256]{1,0:T(8,128)(2,1)} collective-permute-done((bf16[512,256]{1,0:T(8,128)(2,1)S(1)}, bf16[512,256]{1,0:T(8,128)(2,1)}, u32[]{:S(2)}, u32[]{:S(2)}) %collective-permute-start.27) | collective-permute-done | bytes 262176 | tf_op jit(solution)/shard_map/ppermute | solution.py:40
  255.4 1.2 fusion.5
  256.7 1.7 broadcast_select_fusion.1
  258.5 5.7 %collective-permute-done.28 = bf16[512,256]{1,0:T(8,128)(2,1)S(1)} collective-permute-done((bf16[512,256]{1,0:T(8,128)(2,1)S(1)}, bf16[512,256]{1,0:T(8,128)(2,1)S(1)}, u32[]{:S(2)}, u32[]{:S(2)}) %collective-permute-start.28) | collective-permute-done | bytes 262176 | tf_op jit(solution)/shard_map/ppermute | solution.py:40
  264.2 1.9 fusion.11
  266.4 1.8 copy.36
  269.2 4.6 %collective-permute-done.29 = bf16[256,256]{1,0:T(8,128)(2,1)} collective-permute-done((bf16[256,256]{1,0:T(8,128)(2,1)}, bf16[256,256]{1,0:T(8,128)(2,1)}, u32[]{:S(2)}, u32[]{:S(2)}) %collective-permute-start.29) | collective-permute-done | bytes 131104 | tf_op jit(solution)/shard_map/ppermute | solution.py:40
  273.8 1.4 fusion.9
  (192 shorter events, 25.5 us)
Async XLA Ops:
  0.6 9.5 %copy-start = (bf16[1024,512]{1,0:T(8,128)(2,1)S(1)}, bf16[1024,512]{1,0:T(8,128)(2,1)}, u32[]{:S(2)}) copy-start(bf16[1024,512]{1,0:T(8,128)(2,1)} %param.12) | copy-start | bytes 3145732
  1.8 8.2 %copy-start.28 = (f32[256]{0:T(256)}, f32[256]{0:T(256)S(1)}, u32[]{:S(2)}) copy-start(f32[256]{0:T(256)S(1)} %fusion.7) | copy-start | bytes 3076
  1.8 8.2 %copy-start.26 = (f32[256]{0:T(256)}, f32[256]{0:T(256)S(1)}, u32[]{:S(2)}) copy-start(f32[256]{0:T(256)S(1)} %add_rsqrt_fusion.1) | copy-start | bytes 3076
  2.8 53.6 %copy-start.8 = (bf16[256,256]{1,0:T(8,128)(2,1)}, bf16[256,256]{1,0:T(8,128)(2,1)S(1)}, u32[]{:S(2)}) copy-start(bf16[256,256]{1,0:T(8,128)(2,1)S(1)} %fusion.8.refs_0_) | copy-start | bytes 393220
  2.8 42.4 %collective-permute-start.5 = (bf16[256,256]{1,0:T(8,128)(2,1)S(1)}, bf16[256,256]{1,0:T(8,128)(2,1)S(1)}, u32[]{:S(2)}, u32[]{:S(2)}) collective-permute-start(bf16[256,256]{1,0:T(8,128)(2,1)S(1)} %fusion.8.refs_0_), channel_id=1, source_target_pairs={{0,4},{1,5},{2,6},{3,7},{4,0},{5,1},{6,2},{7,3},{8,12},{9,13},{10,... | collective-permute-start | bytes 393224 | tf_op jit(solution)/shard_map/ppermute | solution.py:40
  6.9 68.0 %collective-permute-start.11 = (bf16[256,256]{1,0:T(8,128)(2,1)S(1)}, bf16[256,256]{1,0:T(8,128)(2,1)S(1)}, u32[]{:S(2)}, u32[]{:S(2)}) collective-permute-start(bf16[256,256]{1,0:T(8,128)(2,1)S(1)} %fusion.8.refs_0_), channel_id=1, source_target_pairs={{0,8},{1,9},{2,10},{3,11},{4,12},{5,13},{6,14},{7,15},{8,0},{9,1},... | collective-permute-start | bytes 393224 | tf_op jit(solution)/shard_map/ppermute | solution.py:40
  10.0 8.3 %copy-start.22 = (bf16[512,256]{1,0:T(8,128)(2,1)S(1)}, bf16[512,256]{1,0:T(8,128)(2,1)}, u32[]{:S(2)}) copy-start(bf16[512,256]{1,0:T(8,128)(2,1)} %param.13) | copy-start | bytes 786436
  10.0 20.8 %collective-permute-start = (s32[1,8,128]{2,1,0:T(8,128)S(1)}, s32[1,8,128]{2,1,0:T(8,128)S(1)}, u32[]{:S(2)}, u32[]{:S(2)}) collective-permute-start(s32[1,8,128]{2,1,0:T(8,128)S(1)} %get-tuple-element.67), channel_id=1, source_target_pairs={{0,4},{1,5},{2,6},{3,7},{4,0},{5,1},{6,2},{7,3},{8,12},{9,13},{10,... | collective-permute-start | bytes 12296 | tf_op jit(solution)/shard_map/ppermute | solution.py:40
  27.2 15.0 %copy-start.25 = (s32[4096]{0:T(1024)S(1)}, s32[4096]{0:T(1024)}, u32[]{:S(2)}) copy-start(s32[4096]{0:T(1024)} %param.14) | copy-start | bytes 49156
  27.2 17.7 %copy-start.32 = (s32[256]{0:T(256)S(1)}, s32[256]{0:T(256)}, u32[]{:S(2)}) copy-start(s32[256]{0:T(256)} %constant.119) | copy-start | bytes 3076
  27.2 21.6 %copy-start.30 = (s32[256]{0:T(256)S(1)}, s32[256]{0:T(256)}, u32[]{:S(2)}) copy-start(s32[256]{0:T(256)} %constant.115.clone) | copy-start | bytes 3076
  27.2 21.6 %copy-start.31 = (s32[256]{0:T(256)S(1)}, s32[256]{0:T(256)}, u32[]{:S(2)}) copy-start(s32[256]{0:T(256)} %constant.120) | copy-start | bytes 3076
  30.8 3.7 %collective-permute-start.1 = (s32[2,8,128]{2,1,0:T(8,128)S(1)}, s32[2,8,128]{2,1,0:T(8,128)S(1)}, u32[]{:S(2)}, u32[]{:S(2)}) collective-permute-start(s32[2,8,128]{2,1,0:T(8,128)S(1)} %pad_add_fusion.2), channel_id=1, source_target_pairs={{0,2},{1,3},{2,0},{3,1},{4,6},{5,7},{6,4},{7,5},{8,10},{9,11},{10,... | collective-permute-start | bytes 24584 | tf_op jit(solution)/shard_map/ppermute | solution.py:40
  34.5 3.7 %collective-permute-start.2 = (s32[4,8,128]{2,1,0:T(8,128)S(1)}, s32[4,8,128]{2,1,0:T(8,128)S(1)}, u32[]{:S(2)}, u32[]{:S(2)}) collective-permute-start(s32[4,8,128]{2,1,0:T(8,128)S(1)} %pad_add_fusion.1), channel_id=1, source_target_pairs={{0,1},{1,0},{2,3},{3,2},{4,5},{5,4},{6,7},{7,6},{8,9},{9,8},{10,11... | collective-permute-start | bytes 49160 | tf_op jit(solution)/shard_map/ppermute | solution.py:40
  38.3 3.9 %collective-permute-start.3 = (s32[8,8,128]{2,1,0:T(8,128)S(1)}, s32[8,8,128]{2,1,0:T(8,128)S(1)}, u32[]{:S(2)}, u32[]{:S(2)}) collective-permute-start(s32[8,8,128]{2,1,0:T(8,128)S(1)} %pad_add_fusion), channel_id=1, source_target_pairs={{0,16},{1,17},{2,18},{3,19},{4,20},{5,21},{6,22},{7,23},{8,24},{9,... | collective-permute-start | bytes 98312 | tf_op jit(solution)/shard_map/ppermute | solution.py:40
  42.2 1.3 collective-permute-start.4
  45.3 38.2 %copy-start.12 = (bf16[256,256]{1,0:T(8,128)(2,1)}, bf16[256,256]{1,0:T(8,128)(2,1)S(1)}, u32[]{:S(2)}) copy-start(bf16[256,256]{1,0:T(8,128)(2,1)S(1)} %collective-permute-done.5.refs_1_) | copy-start | bytes 393220
  45.3 8.5 %collective-permute-start.6 = (bf16[512,256]{1,0:T(8,128)(2,1)S(1)}, bf16[512,256]{1,0:T(8,128)(2,1)S(1)}, u32[]{:S(2)}, u32[]{:S(2)}) collective-permute-start(bf16[512,256]{1,0:T(8,128)(2,1)S(1)} %pad_maximum_fusion.4), channel_id=1, source_target_pairs={{0,2},{1,3},{2,0},{3,1},{4,6},{5,7},{6,4},{7,5},{8,10},{9,11},{10,... | collective-permute-start | bytes 786440 | tf_op jit(solution)/shard_map/ppermute | solution.py:40
  47.3 9.1 %collective-permute-start.7 = (bf16[512,256]{1,0:T(8,128)(2,1)S(1)}, bf16[512,256]{1,0:T(8,128)(2,1)S(1)}, u32[]{:S(2)}, u32[]{:S(2)}) collective-permute-start(bf16[512,256]{1,0:T(8,128)(2,1)S(1)} %pad_maximum_fusion.4), channel_id=1, source_target_pairs={{0,1},{1,0},{2,3},{3,2},{4,5},{5,4},{6,7},{7,6},{8,9},{9,8},{10,11... | collective-permute-start | bytes 786440 | tf_op jit(solution)/shard_map/ppermute | solution.py:40
  53.8 29.7 %copy-start.9 = (bf16[512,256]{1,0:T(8,128)(2,1)}, bf16[512,256]{1,0:T(8,128)(2,1)S(1)}, u32[]{:S(2)}) copy-start(bf16[512,256]{1,0:T(8,128)(2,1)S(1)} %collective-permute-done.6.refs_2_) | copy-start | bytes 786436
  53.8 9.2 %collective-permute-start.8 = (bf16[512,256]{1,0:T(8,128)(2,1)S(1)}, bf16[512,256]{1,0:T(8,128)(2,1)S(1)}, u32[]{:S(2)}, u32[]{:S(2)}) collective-permute-start(bf16[512,256]{1,0:T(8,128)(2,1)S(1)} %collective-permute-done.6.refs_2_), channel_id=1, source_target_pairs={{0,16},{1,17},{2,18},{3,19},{4,20},{5,21},{6,22},{7,23},{8,24},{9,... | collective-permute-start | bytes 786440 | tf_op jit(solution)/shard_map/ppermute | solution.py:40
  56.4 9.1 %copy-start.24 = (s32[352]{0:T(512)}, s32[352]{0:T(512)S(1)}, u32[]{:S(2)}) copy-start(s32[352]{0:T(512)S(1)} %get-tuple-element.30.vq) | copy-start | bytes 4228
  56.4 27.1 %copy-start.10 = (bf16[512,256]{1,0:T(8,128)(2,1)}, bf16[512,256]{1,0:T(8,128)(2,1)S(1)}, u32[]{:S(2)}) copy-start(bf16[512,256]{1,0:T(8,128)(2,1)S(1)} %collective-permute-done.7.refs_3_) | copy-start | bytes 786436
  56.5 16.2 %collective-permute-start.9 = (bf16[1024,256]{1,0:T(8,128)(2,1)S(1)}, bf16[1024,256]{1,0:T(8,128)(2,1)S(1)}, u32[]{:S(2)}, u32[]{:S(2)}) collective-permute-start(bf16[1024,256]{1,0:T(8,128)(2,1)S(1)} %pad_maximum_fusion.2), channel_id=1, source_target_pairs={{0,16},{1,17},{2,18},{3,19},{4,20},{5,21},{6,22},{7,23},{8,24},{9,... | collective-permute-start | bytes 1572872 | tf_op jit(solution)/shard_map/ppermute | solution.py:40
  63.0 20.4 %copy-start.11 = (bf16[512,256]{1,0:T(8,128)(2,1)}, bf16[512,256]{1,0:T(8,128)(2,1)S(1)}, u32[]{:S(2)}) copy-start(bf16[512,256]{1,0:T(8,128)(2,1)S(1)} %collective-permute-done.8.refs_4_) | copy-start | bytes 786436
  63.1 10.8 %collective-permute-start.10 = (bf16[1024,256]{1,0:T(8,128)(2,1)S(1)}, bf16[1024,256]{1,0:T(8,128)(2,1)S(1)}, u32[]{:S(2)}, u32[]{:S(2)}) collective-permute-start(bf16[1024,256]{1,0:T(8,128)(2,1)S(1)} %pad_maximum_fusion.3), channel_id=1, source_target_pairs={{0,1},{1,0},{2,3},{3,2},{4,5},{5,4},{6,7},{7,6},{8,9},{9,8},{10,11... | collective-permute-start | bytes 1572872 | tf_op jit(solution)/shard_map/ppermute | solution.py:40
  66.0 9.0 %collective-permute-start.12 = (bf16[256,256]{1,0:T(8,128)(2,1)S(1)}, bf16[256,256]{1,0:T(8,128)(2,1)S(1)}, u32[]{:S(2)}, u32[]{:S(2)}) collective-permute-start(bf16[256,256]{1,0:T(8,128)(2,1)S(1)} %collective-permute-done.5.refs_1_), channel_id=1, source_target_pairs={{0,8},{1,9},{2,10},{3,11},{4,12},{5,13},{6,14},{7,15},{8,0},{9,1},... | collective-permute-start | bytes 393224 | tf_op jit(solution)/shard_map/ppermute | solution.py:40
  72.7 10.8 %copy-start.16 = (bf16[1024,256]{1,0:T(8,128)(2,1)}, bf16[1024,256]{1,0:T(8,128)(2,1)S(1)}, u32[]{:S(2)}) copy-start(bf16[1024,256]{1,0:T(8,128)(2,1)S(1)} %collective-permute-done.9.refs_5_) | copy-start | bytes 1572868
  72.7 8.1 %collective-permute-start.16 = (bf16[1024,256]{1,0:T(8,128)(2,1)S(1)}, bf16[1024,256]{1,0:T(8,128)(2,1)S(1)}, u32[]{:S(2)}, u32[]{:S(2)}) collective-permute-start(bf16[1024,256]{1,0:T(8,128)(2,1)S(1)} %collective-permute-done.9.refs_5_), channel_id=1, source_target_pairs={{0,8},{1,9},{2,10},{3,11},{4,12},{5,13},{6,14},{7,15},{8,0},{9,1},... | collective-permute-start | bytes 1572872 | tf_op jit(solution)/shard_map/ppermute | solution.py:40
  73.9 9.6 %copy-start.17 = (bf16[1024,256]{1,0:T(8,128)(2,1)}, bf16[1024,256]{1,0:T(8,128)(2,1)S(1)}, u32[]{:S(2)}) copy-start(bf16[1024,256]{1,0:T(8,128)(2,1)S(1)} %collective-permute-done.10.refs_6_) | copy-start | bytes 1572868
  73.9 6.9 %collective-permute-start.17 = (bf16[1024,256]{1,0:T(8,128)(2,1)S(1)}, bf16[1024,256]{1,0:T(8,128)(2,1)S(1)}, u32[]{:S(2)}, u32[]{:S(2)}) collective-permute-start(bf16[1024,256]{1,0:T(8,128)(2,1)S(1)} %collective-permute-done.10.refs_6_), channel_id=1, source_target_pairs={{0,8},{1,9},{2,10},{3,11},{4,12},{5,13},{6,14},{7,15},{8,0},{9,1},... | collective-permute-start | bytes 1572872 | tf_op jit(solution)/shard_map/ppermute | solution.py:40
  74.5 6.3 %collective-permute-start.13 = (bf16[512,256]{1,0:T(8,128)(2,1)S(1)}, bf16[512,256]{1,0:T(8,128)(2,1)}, u32[]{:S(2)}, u32[]{:S(2)}) collective-permute-start(bf16[512,256]{1,0:T(8,128)(2,1)S(1)} %collective-permute-done.6.refs_2_), channel_id=1, source_target_pairs={{0,8},{1,9},{2,10},{3,11},{4,12},{5,13},{6,14},{7,15},{8,0},{9,1},... | collective-permute-start | bytes 786440 | tf_op jit(solution)/shard_map/ppermute | solution.py:40
  75.0 8.6 %copy-start.20 = (bf16[256,256]{1,0:T(8,128)(2,1)}, bf16[256,256]{1,0:T(8,128)(2,1)S(1)}, u32[]{:S(2)}) copy-start(bf16[256,256]{1,0:T(8,128)(2,1)S(1)} %collective-permute-done.11.refs_7_) | copy-start | bytes 393220
  75.0 5.8 %collective-permute-start.14 = (bf16[512,256]{1,0:T(8,128)(2,1)S(1)}, bf16[512,256]{1,0:T(8,128)(2,1)}, u32[]{:S(2)}, u32[]{:S(2)}) collective-permute-start(bf16[512,256]{1,0:T(8,128)(2,1)S(1)} %collective-permute-done.7.refs_3_), channel_id=1, source_target_pairs={{0,8},{1,9},{2,10},{3,11},{4,12},{5,13},{6,14},{7,15},{8,0},{9,1},... | collective-permute-start | bytes 786440 | tf_op jit(solution)/shard_map/ppermute | solution.py:40
  75.0 8.5 %copy-start.21 = (bf16[256,256]{1,0:T(8,128)(2,1)}, bf16[256,256]{1,0:T(8,128)(2,1)S(1)}, u32[]{:S(2)}) copy-start(bf16[256,256]{1,0:T(8,128)(2,1)S(1)} %collective-permute-done.12.refs_8_) | copy-start | bytes 393220
  75.0 5.7 %collective-permute-start.15 = (bf16[512,256]{1,0:T(8,128)(2,1)S(1)}, bf16[512,256]{1,0:T(8,128)(2,1)}, u32[]{:S(2)}, u32[]{:S(2)}) collective-permute-start(bf16[512,256]{1,0:T(8,128)(2,1)S(1)} %collective-permute-done.8.refs_4_), channel_id=1, source_target_pairs={{0,8},{1,9},{2,10},{3,11},{4,12},{5,13},{6,14},{7,15},{8,0},{9,1},... | collective-permute-start | bytes 786440 | tf_op jit(solution)/shard_map/ppermute | solution.py:40
  101.6 8.1 %collective-permute-start.18 = (f32[128,128]{1,0:T(8,128)S(1)}, f32[128,128]{1,0:T(8,128)S(1)}, u32[]{:S(2)}, u32[]{:S(2)}) collective-permute-start(f32[128,128]{1,0:T(8,128)S(1)} %constant_dynamic-update-slice_fusion.5), channel_id=1, source_target_pairs={{0,8},{1,9},{2,10},{3,11},{4,12},{5,13},{6,14},{7,15},{8,0},{9,1},... | collective-permute-start | bytes 196616 | tf_op jit(solution)/shard_map/ppermute | solution.py:40
  109.7 4.4 %collective-permute-start.19 = (f32[128,128]{1,0:T(8,128)S(1)}, f32[128,128]{1,0:T(8,128)S(1)}, u32[]{:S(2)}, u32[]{:S(2)}) collective-permute-start(f32[128,128]{1,0:T(8,128)S(1)} %add.239), channel_id=1, source_target_pairs={{0,16},{1,17},{2,18},{3,19},{4,20},{5,21},{6,22},{7,23},{8,24},{9,... | collective-permute-start | bytes 196616 | tf_op jit(solution)/shard_map/ppermute | solution.py:40
  114.1 4.3 %collective-permute-start.20 = (f32[128,128]{1,0:T(8,128)S(1)}, f32[128,128]{1,0:T(8,128)S(1)}, u32[]{:S(2)}, u32[]{:S(2)}) collective-permute-start(f32[128,128]{1,0:T(8,128)S(1)} %add.240), channel_id=1, source_target_pairs={{0,1},{1,0},{2,3},{3,2},{4,5},{5,4},{6,7},{7,6},{8,9},{9,8},{10,11... | collective-permute-start | bytes 196616 | tf_op jit(solution)/shard_map/ppermute | solution.py:40
  118.5 4.3 %collective-permute-start.21 = (f32[128,128]{1,0:T(8,128)S(1)}, f32[128,128]{1,0:T(8,128)S(1)}, u32[]{:S(2)}, u32[]{:S(2)}) collective-permute-start(f32[128,128]{1,0:T(8,128)S(1)} %add.241), channel_id=1, source_target_pairs={{0,2},{1,3},{2,0},{3,1},{4,6},{5,7},{6,4},{7,5},{8,10},{9,11},{10,... | collective-permute-start | bytes 196616 | tf_op jit(solution)/shard_map/ppermute | solution.py:40
  122.8 5.4 %collective-permute-start.22 = (f32[128,128]{1,0:T(8,128)S(1)}, f32[128,128]{1,0:T(8,128)S(1)}, u32[]{:S(2)}, u32[]{:S(2)}) collective-permute-start(f32[128,128]{1,0:T(8,128)S(1)} %add.242), channel_id=1, source_target_pairs={{0,4},{1,5},{2,6},{3,7},{4,0},{5,1},{6,2},{7,3},{8,12},{9,13},{10,... | collective-permute-start | bytes 196616 | tf_op jit(solution)/shard_map/ppermute | solution.py:40
  173.7 5.9 %collective-permute-start.30 = (bf16[640,512]{0,1:T(8,128)(2,1)S(1)}, bf16[640,512]{0,1:T(8,128)(2,1)S(1)}, u32[]{:S(2)}, u32[]{:S(2)}) collective-permute-start(bf16[640,512]{0,1:T(8,128)(2,1)S(1)} %dynamic-slice_convert_fusion), channel_id=1, source_target_pairs={{0,8},{1,9},{2,10},{3,11},{4,12},{5,13},{6,14},{7,15},{8,0},{9,1},... | collective-permute-start | bytes 1966088 | tf_op jit(solution)/shard_map/ppermute | solution.py:40
  177.8 43.2 %collective-permute-start.23 = (bf16[4096,256]{1,0:T(8,128)(2,1)}, bf16[4096,256]{1,0:T(8,128)(2,1)}, u32[]{:S(2)}, u32[]{:S(2)}) collective-permute-start(bf16[4096,256]{1,0:T(8,128)(2,1)} %get-tuple-element.14), channel_id=1, source_target_pairs={{0,8},{1,9},{2,10},{3,11},{4,12},{5,13},{6,14},{7,15},{8,0},{9,1},... | collective-permute-start | bytes 6291464 | tf_op jit(solution)/shard_map/ppermute | solution.py:40
  181.4 10.2 %collective-permute-start.33 = (bf16[160,512]{0,1:T(8,128)(2,1)S(1)}, bf16[160,512]{0,1:T(8,128)(2,1)S(1)}, u32[]{:S(2)}, u32[]{:S(2)}) collective-permute-start(bf16[160,512]{0,1:T(8,128)(2,1)S(1)} %get-tuple-element.50), channel_id=1, source_target_pairs={{0,17},{1,16},{2,19},{3,18},{4,21},{5,20},{6,23},{7,22},{8,25},{9,... | collective-permute-start | bytes 491528 | tf_op jit(solution)/shard_map/ppermute | solution.py:40
  181.5 14.3 %collective-permute-start.32 = (bf16[160,512]{0,1:T(8,128)(2,1)S(1)}, bf16[160,512]{0,1:T(8,128)(2,1)S(1)}, u32[]{:S(2)}, u32[]{:S(2)}) collective-permute-start(bf16[160,512]{0,1:T(8,128)(2,1)S(1)} %get-tuple-element.51), channel_id=1, source_target_pairs={{0,1},{1,0},{2,3},{3,2},{4,5},{5,4},{6,7},{7,6},{8,9},{9,8},{10,11... | collective-permute-start | bytes 491528 | tf_op jit(solution)/shard_map/ppermute | solution.py:40
  181.6 14.2 %collective-permute-start.31 = (bf16[160,512]{0,1:T(8,128)(2,1)S(1)}, bf16[160,512]{0,1:T(8,128)(2,1)S(1)}, u32[]{:S(2)}, u32[]{:S(2)}) collective-permute-start(bf16[160,512]{0,1:T(8,128)(2,1)S(1)} %get-tuple-element.49), channel_id=1, source_target_pairs={{0,16},{1,17},{2,18},{3,19},{4,20},{5,21},{6,22},{7,23},{8,24},{9,... | collective-permute-start | bytes 491528 | tf_op jit(solution)/shard_map/ppermute | solution.py:40
  196.0 7.8 %collective-permute-start.34 = (bf16[160,512]{0,1:T(8,128)(2,1)S(1)}, bf16[160,512]{0,1:T(8,128)(2,1)S(1)}, u32[]{:S(2)}, u32[]{:S(2)}) collective-permute-start(bf16[160,512]{0,1:T(8,128)(2,1)S(1)} %add_convert_fusion.2), channel_id=1, source_target_pairs={{0,2},{1,3},{2,0},{3,1},{4,6},{5,7},{6,4},{7,5},{8,10},{9,11},{10,... | collective-permute-start | bytes 491528 | tf_op jit(solution)/shard_map/ppermute | solution.py:40
  203.9 13.4 %collective-permute-start.35 = (bf16[160,512]{0,1:T(8,128)(2,1)S(1)}, bf16[160,512]{0,1:T(8,128)(2,1)S(1)}, u32[]{:S(2)}, u32[]{:S(2)}) collective-permute-start(bf16[160,512]{0,1:T(8,128)(2,1)S(1)} %add_convert_fusion.1), channel_id=1, source_target_pairs={{0,4},{1,5},{2,6},{3,7},{4,0},{5,1},{6,2},{7,3},{8,12},{9,13},{10,... | collective-permute-start | bytes 491528 | tf_op jit(solution)/shard_map/ppermute | solution.py:40
  217.4 11.7 %collective-permute-start.36 = (bf16[160,512]{0,1:T(8,128)(2,1)S(1)}, bf16[160,512]{0,1:T(8,128)(2,1)S(1)}, u32[]{:S(2)}, u32[]{:S(2)}) collective-permute-start(bf16[160,512]{0,1:T(8,128)(2,1)S(1)} %add_convert_fusion), channel_id=1, source_target_pairs={{0,17},{1,16},{2,19},{3,18},{4,21},{5,20},{6,23},{7,22},{8,25},{9,... | collective-permute-start | bytes 491528 | tf_op jit(solution)/shard_map/ppermute | solution.py:40
  219.6 12.7 %collective-permute-start.37 = (bf16[160,512]{0,1:T(8,128)(2,1)S(1)}, bf16[160,512]{0,1:T(8,128)(2,1)S(1)}, u32[]{:S(2)}, u32[]{:S(2)}) collective-permute-start(bf16[160,512]{0,1:T(8,128)(2,1)S(1)} %add_convert_fusion), channel_id=1, source_target_pairs={{0,1},{1,0},{2,3},{3,2},{4,5},{5,4},{6,7},{7,6},{8,9},{9,8},{10,11... | collective-permute-start | bytes 491528 | tf_op jit(solution)/shard_map/ppermute | solution.py:40
  219.7 13.6 %collective-permute-start.38 = (bf16[160,512]{0,1:T(8,128)(2,1)S(1)}, bf16[160,512]{0,1:T(8,128)(2,1)}, u32[]{:S(2)}, u32[]{:S(2)}) collective-permute-start(bf16[160,512]{0,1:T(8,128)(2,1)S(1)} %add_convert_fusion), channel_id=1, source_target_pairs={{0,16},{1,17},{2,18},{3,19},{4,20},{5,21},{6,22},{7,23},{8,24},{9,... | collective-permute-start | bytes 491528 | tf_op jit(solution)/shard_map/ppermute | solution.py:40
  226.4 17.0 %collective-permute-start.26 = (bf16[1024,256]{1,0:T(8,128)(2,1)S(1)}, bf16[1024,256]{1,0:T(8,128)(2,1)S(1)}, u32[]{:S(2)}, u32[]{:S(2)}) collective-permute-start(bf16[1024,256]{1,0:T(8,128)(2,1)S(1)} %get-tuple-element.46), channel_id=1, source_target_pairs={{0,1},{1,0},{2,3},{3,2},{4,5},{5,4},{6,7},{7,6},{8,9},{9,8},{10,11... | collective-permute-start | bytes 1572872 | tf_op jit(solution)/shard_map/ppermute | solution.py:40
  227.9 15.6 %collective-permute-start.24 = (bf16[1024,256]{1,0:T(8,128)(2,1)S(1)}, bf16[1024,256]{1,0:T(8,128)(2,1)}, u32[]{:S(2)}, u32[]{:S(2)}) collective-permute-start(bf16[1024,256]{1,0:T(8,128)(2,1)S(1)} %get-tuple-element.45), channel_id=1, source_target_pairs={{0,16},{1,17},{2,18},{3,19},{4,20},{5,21},{6,22},{7,23},{8,24},{9,... | collective-permute-start | bytes 1572872 | tf_op jit(solution)/shard_map/ppermute | solution.py:40
  235.5 21.2 %collective-permute-start.39 = (bf16[640,512]{0,1:T(8,128)(2,1)}, bf16[640,512]{0,1:T(8,128)(2,1)}, u32[]{:S(2)}, u32[]{:S(2)}) collective-permute-start(bf16[640,512]{0,1:T(8,128)(2,1)} %pad_maximum_fusion.1), channel_id=1, source_target_pairs={{0,8},{1,9},{2,10},{3,11},{4,12},{5,13},{6,14},{7,15},{8,0},{9,1},... | collective-permute-start | bytes 1966088 | tf_op jit(solution)/shard_map/ppermute | solution.py:40
  244.6 19.5 %copy-start.7 = (f32[1024,256]{1,0:T(8,128)}, f32[1024,256]{1,0:T(8,128)S(1)}, u32[]{:S(2)}) copy-start(f32[1024,256]{1,0:T(8,128)S(1)} %convert_element_type.137) | copy-start | bytes 3145732
  247.0 8.4 %collective-permute-start.27 = (bf16[512,256]{1,0:T(8,128)(2,1)S(1)}, bf16[512,256]{1,0:T(8,128)(2,1)}, u32[]{:S(2)}, u32[]{:S(2)}) collective-permute-start(bf16[512,256]{1,0:T(8,128)(2,1)S(1)} %get-tuple-element.44), channel_id=1, source_target_pairs={{0,16},{1,17},{2,18},{3,19},{4,20},{5,21},{6,22},{7,23},{8,24},{9,... | collective-permute-start | bytes 786440 | tf_op jit(solution)/shard_map/ppermute | solution.py:40
  248.8 9.6 %collective-permute-start.25 = (bf16[512,256]{1,0:T(8,128)(2,1)}, bf16[512,256]{1,0:T(8,128)(2,1)S(1)}, u32[]{:S(2)}, u32[]{:S(2)}) collective-permute-start(bf16[512,256]{1,0:T(8,128)(2,1)} %get-tuple-element.43), channel_id=1, source_target_pairs={{0,1},{1,0},{2,3},{3,2},{4,5},{5,4},{6,7},{7,6},{8,9},{9,8},{10,11... | collective-permute-start | bytes 786440 | tf_op jit(solution)/shard_map/ppermute | solution.py:40
  256.6 7.5 %collective-permute-start.28 = (bf16[512,256]{1,0:T(8,128)(2,1)S(1)}, bf16[512,256]{1,0:T(8,128)(2,1)S(1)}, u32[]{:S(2)}, u32[]{:S(2)}) collective-permute-start(bf16[512,256]{1,0:T(8,128)(2,1)S(1)} %fusion.5), channel_id=1, source_target_pairs={{0,2},{1,3},{2,0},{3,1},{4,6},{5,7},{6,4},{7,5},{8,10},{9,11},{10,... | collective-permute-start | bytes 786440 | tf_op jit(solution)/shard_map/ppermute | solution.py:40
  258.5 7.6 %copy-start.13 = (f32[512,256]{1,0:T(8,128)}, f32[512,256]{1,0:T(8,128)S(1)}, u32[]{:S(2)}) copy-start(f32[512,256]{1,0:T(8,128)S(1)} %convert_element_type.139) | copy-start | bytes 1572868
  266.0 7.7 %collective-permute-start.29 = (bf16[256,256]{1,0:T(8,128)(2,1)}, bf16[256,256]{1,0:T(8,128)(2,1)}, u32[]{:S(2)}, u32[]{:S(2)}) collective-permute-start(bf16[256,256]{1,0:T(8,128)(2,1)} %fusion.11), channel_id=1, source_target_pairs={{0,4},{1,5},{2,6},{3,7},{4,0},{5,1},{6,2},{7,3},{8,12},{9,13},{10,... | collective-permute-start | bytes 393224 | tf_op jit(solution)/shard_map/ppermute | solution.py:40
  266.1 7.7 %copy-start.15 = (bf16[256,256]{1,0:T(8,128)(2,1)S(1)}, bf16[256,256]{1,0:T(8,128)(2,1)}, u32[]{:S(2)}) copy-start(bf16[256,256]{1,0:T(8,128)(2,1)} %param.15) | copy-start | bytes 393220
  266.1 10.0 %copy-start.1 = (bf16[1024,512]{1,0:T(8,128)(2,1)S(1)}, bf16[1024,512]{1,0:T(8,128)(2,1)}, u32[]{:S(2)}) copy-start(bf16[1024,512]{1,0:T(8,128)(2,1)} %param.12) | copy-start | bytes 3145732
  266.3 8.8 %copy-start.29 = (f32[256]{0:T(256)S(1)}, f32[256]{0:T(256)}, u32[]{:S(2)}) copy-start(f32[256]{0:T(256)} %copy-done.28) | copy-start | bytes 3076
  266.4 8.8 %copy-start.27 = (f32[256]{0:T(256)S(1)}, f32[256]{0:T(256)}, u32[]{:S(2)}) copy-start(f32[256]{0:T(256)} %copy-done.26) | copy-start | bytes 3076
  (9 other events, 26.3 us)

commit v2 on v1

v2 whole, which is shorter than its diff:
```python
import functools

import jax
import jax.numpy as jnp
import numpy as np
from jax import lax
from jax.experimental import pallas as pl
from jax.experimental.pallas import tpu as pltpu
from jax.sharding import PartitionSpec as P

BLK = 128
NQ = 8
QB = 16
SUB = 4
UNROLL = 4
TILE = 512
HEAD = 16

LOGIT_SCALE = 20.0
LOSS_SCALE = 4096.0
NORM_EPSILON = 1e-06

AXES = ("user", "item")
F32 = jnp.float32
BF16 = jnp.bfloat16
I32 = jnp.int32


class Links:
    def __init__(self):
        users = lax.axis_size("user")
        items = lax.axis_size("item")
        self.devices = users * items
        item_bits = items.bit_length() - 1
        user_bits = users.bit_length() - 1
        self.y = list(range(item_bits - 2))
        self.z = [item_bits - 1, item_bits - 2]
        self.core = item_bits
        self.x = list(range(item_bits + 1, item_bits + user_bits))

    def swap(self, value, mask):
        pairs = [(d, d ^ mask) for d in range(self.devices)]
        return lax.ppermute(value, AXES, pairs)


def join(parts):
    return parts[0] if len(parts) == 1 else jnp.concatenate(parts, axis=0)


def gather_plan(links):
    masks = [[0]]
    steps = []

    def add(bit, sources):
        steps.append((1 << bit, list(sources)))
        masks.append([m ^ (1 << bit) for s in sources for m in masks[s]])
        return len(masks) - 1

    base = [0]
    for bit in links.z:
        base.append(add(bit, base))
    first, second = base[:-1], base[-1:]
    for bit_a, bit_b in zip(links.y + links.x, links.x + links.y):
        new_a = add(bit_a, first)
        new_b = add(bit_b, second)
        first, second = first + [new_a], second + [new_b]
    return masks, steps


def piece_copies(pieces, scratch, sems, start, rows, count):
    copies = []
    for piece in pieces:
        for first in range(0, piece.shape[0], count):
            place = len(copies)
            copies.append(
                pltpu.make_async_copy(
                    piece.at[pl.ds(first + start, rows), :],
                    scratch.at[pl.ds(place * rows, rows), :],
                    sems.at[place],
                )
            )
    return copies


def tower_kernel(feats, first_t, second_t, hidden_t, tower, vectors):
    linear = lax.dot_general(
        first_t[...], feats[...], (((1,), (1,)), ((), ())), preferred_element_type=F32
    )
    hidden = jnp.maximum(linear, 0.0).astype(BF16)
    hidden_t[...] = hidden
    out = jnp.dot(second_t[...], hidden, preferred_element_type=F32).T
    tower[...] = out
    norm = lax.rsqrt(jnp.sum(out * out, axis=1, keepdims=True) + NORM_EPSILON)
    vectors[...] = (out * norm).astype(BF16)


class Plan:
    def __init__(self, ref, spots, tiles):
        self.ref = ref
        self.spots = spots
        self.tiles = tiles
        self.chunk_base = 2 * spots
        self.tile_base = self.chunk_base + spots // SUB
        self.size = self.tile_base + tiles + 2

    def ul(self, q):
        return self.ref[q] & 0xFFFF

    def tl(self, q):
        return self.ref[q] >> 16

    def kq(self, q):
        return self.ref[self.spots + q] & 0xFFFF

    def vq(self, q):
        return self.ref[self.spots + q] >> 16

    def cblk(self, c):
        return self.ref[self.chunk_base + c]

    def starts(self, t):
        return self.ref[self.tile_base + t]

    def nch(self):
        return self.ref[self.tile_base + self.tiles]


def plan_kernel(n_pieces, capacity, tile_blocks, sizes, where, masks, *refs):
    pieces = refs[:n_pieces]
    out, positions, raw, wide_a, wide_b, picked, table, count, cursor, sems = refs[n_pieces:]
    layout = Plan(out, *sizes)
    spots = layout.spots
    blocks = count.shape[0] - 1
    devices = picked.shape[0] // 2
    lane, me, half = where[0], where[1], where[2]
    per = raw.shape[0] // devices
    width = raw.shape[1]
    copies = piece_copies(pieces, raw, sems, width, per, width + per)
    for copy in copies:
        copy.start()

    def clear(b, carry):
        count[b] = 0
        return carry

    lax.fori_loop(0, blocks + 1, clear, 0)
    for copy in copies:
        copy.wait()
    wide_a[...] = raw[:, :BLK].astype(F32)
    wide_b[...] = raw[:, BLK:].astype(F32)
    for field in range(2):
        rows = pl.ds(field, devices, stride=per)
        side = jnp.where(half > 0, wide_b[rows, :], wide_a[rows, :])
        picked[pl.ds(field * devices, devices), :] = side.astype(I32)
    move = pltpu.make_async_copy(picked, table, sems.at[0])
    move.start()
    for i, wide in enumerate((wide_a, wide_b)):
        high = wide[pl.ds(2, devices, stride=per), :]
        low = wide[pl.ds(3, devices, stride=per), :]
        positions[pl.ds(i, devices, stride=2), :] = (high * BLK + low).astype(I32)
    move.wait()

    def tally(j, carry):
        for k in range(capacity):
            valid = table[j, lane + k] > 0
            b = jnp.where(valid, table[devices + j, lane + k], blocks)
            count[b] += 1
        return carry

    lax.fori_loop(0, devices, tally, 0)

    def blank(q):
        out[q] = 0
        out[spots + q] = 0

    def place(b, start):
        n = count[b]
        chunks = (n + SUB - 1) // SUB
        cursor[b] = start * SUB

        def name(c, carry):
            out[layout.chunk_base + c] = b
            for i in range(SUB):
                blank(c * SUB + i)
            return carry

        lax.fori_loop(start, start + chunks, name, 0)

        @pl.when(b % tile_blocks == 0)
        def _():
            out[layout.tile_base + b // tile_blocks] = start

        return start + chunks

    total = lax.fori_loop(0, blocks, place, 0)
    out[layout.tile_base + layout.tiles] = total
    for extra in range(UNROLL):
        out[layout.chunk_base + total + extra] = 0
        for i in range(SUB):
            blank((total + extra) * SUB + i)

    def settle(j, carry):
        device = masks[j] ^ me
        fixed = j * NQ + device * (NQ << 16)
        for k in range(capacity):
            code = table[j, lane + k]
            valid = code > 0
            b = jnp.where(valid, table[devices + j, lane + k], blocks)
            q = jnp.where(valid, cursor[b], spots - 1)
            cursor[b] = q + 1
            request = jnp.maximum(code - 1, 0)
            in_list = request // QB
            out[q] = jnp.where(valid, fixed + in_list * 65537, 0)
            out[spots + q] = jnp.where(valid, request % QB + 65536, 0)
        return carry

    lax.fori_loop(0, devices, settle, 0)


def spread(packed, out, group):
    lane_group = lax.broadcasted_iota(I32, (1, BLK), 1) // group
    for i in range(SUB):
        part = jnp.where(lane_group == i, packed, jnp.zeros_like(packed))
        part = part + pltpu.roll(part, 2 * group, axis=1)
        out[pl.ds(i, packed.shape[0], stride=SUB), :] = part + pltpu.roll(part, group, axis=1)


def score_kernel(n_pieces, group, sizes, plan_ref, *refs):
    plan = Plan(plan_ref, *sizes)
    pieces = refs[:n_pieces]
    vectors, logs, positions, exp_out, loc_out, totals_out, pos_out = refs[n_pieces : n_pieces + 7]
    users, p_rep, t_acc, p_acc, sems = refs[n_pieces + 7 :]
    copies = piece_copies(pieces, users, sems, 0, NQ * group, NQ * group + HEAD)
    for copy in copies:
        copy.start()
    t_acc[...] = jnp.zeros_like(t_acc)
    p_acc[...] = jnp.zeros_like(p_acc)
    spread(positions[...], p_rep, group)
    rows_iota = lax.broadcasted_iota(I32, (BLK, BLK), 0)
    lane_group = lax.broadcasted_iota(I32, (1, BLK), 1) // group
    for copy in copies:
        copy.wait()

    def chunk(c):
        first = pl.multiple_of(plan.cblk(c) * BLK, BLK)
        block = vectors[pl.ds(first, BLK), :]
        members = jnp.concatenate(
            [users[pl.ds(pl.multiple_of(plan.ul(c * SUB + i) * group, group), group), :] for i in range(SUB)],
            axis=0,
        )
        dots = lax.dot_general(block, members, (((1,), (1,)), ((), ())), preferred_element_type=F32)
        scores = LOGIT_SCALE * dots - logs[pl.ds(first, BLK), :]
        exp_scores = jnp.exp(scores)
        exp_out[pl.ds(pl.multiple_of(c * BLK, BLK), BLK), :] = exp_scores
        loc = jnp.full((1, BLK), -1, I32)
        masks = []
        for i in range(SUB):
            spot = c * SUB + i
            mask = jnp.logical_and(lane_group == i, plan.vq(spot) > 0)
            masks.append(mask)
            loc = jnp.where(mask, p_rep[pl.ds(plan.ul(spot), 1), :] - plan.kq(spot) * BLK, loc)
        loc_out[pl.ds(c, 1), :] = loc
        chosen = jnp.where(rows_iota == loc, scores, 0.0)
        return masks, jnp.sum(exp_scores, axis=0, keepdims=True), jnp.sum(chosen, axis=0, keepdims=True)

    def step(q, carry):
        done = [chunk(q * UNROLL + j) for j in range(UNROLL)]
        for j, (masks, total, chosen) in enumerate(done):
            for i in range(SUB):
                row = plan.tl((q * UNROLL + j) * SUB + i)
                t_acc[pl.ds(row, 1), :] += jnp.where(masks[i], total, 0.0)
                p_acc[pl.ds(row, 1), :] += jnp.where(masks[i], chosen, 0.0)
        return carry

    lax.fori_loop(0, (plan.nch() + UNROLL - 1) // UNROLL, step, 0)
    packed_rows = totals_out.shape[0]
    for acc, out in ((t_acc, totals_out), (p_acc, pos_out)):
        value = acc[...]
        both = value + pltpu.roll(value, 2 * group, axis=1)
        acc[...] = both + pltpu.roll(both, group, axis=1)
        packed = jnp.zeros((packed_rows, BLK), F32)
        for i in range(SUB):
            packed += jnp.where(lane_group == i, acc[pl.ds(i, packed_rows, stride=SUB), :], 0.0)
        out[...] = packed


def vector_kernel(group, scale, columns, sizes, plan_ref, *refs):
    plan = Plan(plan_ref, *sizes)
    vectors, exp_in, loc, totals, keep_out, send_out, grad_out, t_rep, v_acc, sem = refs
    v_acc[...] = jnp.zeros_like(v_acc)
    rows_iota = lax.broadcasted_iota(I32, (BLK, BLK), 0)
    lane_group = lax.broadcasted_iota(I32, (1, BLK), 1) // group
    spread(scale / totals[...], t_rep, group)
    low, high = columns

    def chunk(c):
        first = pl.multiple_of(plan.cblk(c) * BLK, BLK)
        weight = jnp.zeros((1, BLK), F32)
        for i in range(SUB):
            keep = jnp.logical_and(lane_group == i, plan.vq(c * SUB + i) > 0)
            weight += jnp.where(keep, t_rep[pl.ds(plan.tl(c * SUB + i), 1), :], 0.0)
        is_positive = rows_iota == loc[pl.ds(c, 1), :]
        here = pl.multiple_of(c * BLK, BLK)
        grad = (exp_in[pl.ds(here, BLK), :] * weight - jnp.where(is_positive, scale, 0.0)).astype(BF16)
        grad_out[pl.ds(here, BLK), :] = grad
        block = vectors[pl.ds(first, BLK), low:high]
        return lax.dot_general(grad, block, (((0,), (0,)), ((), ())), preferred_element_type=F32)

    def step(q, carry):
        parts = [chunk(q * UNROLL + j) for j in range(UNROLL)]
        for j in range(UNROLL):
            for i in range(SUB):
                start = pl.multiple_of(plan.ul((q * UNROLL + j) * SUB + i) * group, group)
                v_acc[pl.ds(start, group), :] += parts[j][i * group : (i + 1) * group]
        return carry

    lax.fori_loop(0, (plan.nch() + UNROLL - 1) // UNROLL, step, 0)
    half = v_acc.shape[0] // 2
    copy = pltpu.make_async_copy(v_acc.at[pl.ds(0, half), :], keep_out, sem)
    copy.start()
    send_out[...] = (LOGIT_SCALE * v_acc[pl.ds(half, half), :]).astype(BF16)
    copy.wait()


def item_kernel(n_pieces, group, tile_blocks, sizes, plan_ref, *refs):
    plan = Plan(plan_ref, *sizes)
    pieces = refs[:n_pieces]
    tower, grads, out_gradient, users, items, sems = refs[n_pieces:]
    tile = pl.program_id(0)

    @pl.when(tile == 0)
    def _():
        copies = piece_copies(pieces, users, sems, 0, NQ * group, NQ * group + HEAD)
        for copy in copies:
            copy.start()
        for copy in copies:
            copy.wait()

    items[...] = jnp.zeros_like(items)
    end = plan.starts(tile + 1)

    def chunk(c):
        members = jnp.concatenate(
            [users[pl.ds(pl.multiple_of(plan.ul(c * SUB + i) * group, group), group), :] for i in range(SUB)],
            axis=0,
        )
        grad = grads[pl.ds(pl.multiple_of(c * BLK, BLK), BLK), :]
        return jnp.dot(grad, members, preferred_element_type=F32)

    def step(q, carry):
        base = plan.starts(tile) + q * UNROLL
        parts = [chunk(base + j) for j in range(UNROLL)]
        for j in range(UNROLL):
            block = jnp.where(base + j < end, plan.cblk(base + j) - tile * tile_blocks, tile_blocks)
            first = pl.multiple_of(block * BLK, BLK)
            items[pl.ds(first, BLK), :] += parts[j]
        return carry

    lax.fori_loop(0, (end - plan.starts(tile) + UNROLL - 1) // UNROLL, step, 0)
    out = tower[...]
    gradient = LOGIT_SCALE * items[pl.ds(0, tile_blocks * BLK), :]
    norm = lax.rsqrt(jnp.sum(out * out, axis=1, keepdims=True) + NORM_EPSILON)
    projection = jnp.sum(out * gradient, axis=1, keepdims=True)
    out_gradient[...] = (gradient * norm - out * (projection * norm * norm * norm)).astype(BF16)


def weight_kernel(feats, hidden_t, second, out_gradient, first_out, second_out, first_t):
    tile = pl.program_id(0)

    @pl.when(tile == 0)
    def _():
        first_t[...] = jnp.zeros_like(first_t)
        second_out[...] = jnp.zeros_like(second_out)

    grad = out_gradient[...]
    hidden = hidden_t[...]
    second_out[...] += jnp.dot(hidden, grad, preferred_element_type=F32)
    act = lax.dot_general(second[...], grad, (((1,), (1,)), ((), ())), preferred_element_type=F32)
    act = jnp.where(hidden > 0, act, 0.0).astype(BF16)
    first_t[...] += jnp.dot(act, feats[...], preferred_element_type=F32)

    @pl.when(tile == pl.num_programs(0) - 1)
    def _():
        first_out[...] = first_t[...].T


def limit(mib):
    return pltpu.CompilerParams(vmem_limit_bytes=mib * 1024 * 1024)


def busy(micros):
    return pl.CostEstimate(flops=micros * 10**9, bytes_accessed=micros * 3 * 10**6, transcendentals=0)


def any_spec():
    return pl.BlockSpec(memory_space=pl.ANY)


def smem_spec():
    return pl.BlockSpec(memory_space=pltpu.SMEM)


def vmem_spec():
    return pl.BlockSpec(memory_space=pltpu.VMEM)


def body(
    item_feats, first_weight, second_weight, counts, user_embed, list_owner, list_slot, positive
):
    links = Links()
    devices = links.devices
    me = lax.axis_index(AXES)
    item_rows, _ = item_feats.shape
    own_blocks = item_rows // BLK
    user_rows, emb = user_embed.shape
    requests = list_slot.shape[0]
    capacity = 2 * requests // devices
    group = user_rows // NQ
    all_users = user_rows * devices
    slots = devices * capacity
    lists = devices * NQ
    core = 1 << links.core

    user_float = user_embed.astype(F32)
    user_norm = lax.rsqrt(jnp.sum(user_float * user_float, axis=1, keepdims=True) + NORM_EPSILON)
    user_vector = (user_float * user_norm).astype(BF16)

    masks, steps = gather_plan(links)
    order = [m for piece in masks for m in piece]
    order = order + [m ^ core for m in order]

    owners = list_owner[:, 0]
    same_owner = owners[:, None] == owners[None, :]
    request = jnp.arange(requests, dtype=I32)
    rank = jnp.sum((same_owner & (request[None, :] < request[:, None])).astype(I32), axis=1)
    position = owners * capacity + rank
    hit = position[:, None] == jnp.arange(slots, dtype=I32)[None, :]
    request_code = jnp.sum(jnp.where(hit, request[:, None] + 1, 0), axis=0)
    slot_code = jnp.sum(jnp.where(hit, list_slot[:, None], 0), axis=0)
    head = jnp.stack([request_code, slot_code, positive // BLK, positive % BLK])
    head = jnp.pad(head, ((0, HEAD - head.shape[0]), (0, 0))).astype(BF16)

    n_z = len(links.z)
    logs = jnp.log(counts.astype(F32)).astype(BF16).astype(F32)
    logs = jnp.broadcast_to(logs[:, None], (item_rows, BLK))
    first_t, second_t = first_weight.T, second_weight.T
    mask = steps[0][0]
    arrived, arrived_head = links.swap(user_vector, mask), links.swap(head, mask)
    arrived, logs, first_t, second_t = lax.optimization_barrier((arrived, logs, first_t, second_t))
    pieces = [join([user_vector, head]), join([arrived, arrived_head])]
    for index in range(1, n_z):
        mask, sources = steps[index]
        pieces.append(links.swap(join([pieces[s] for s in sources]), mask))
    for index in range(n_z, len(steps), 2):
        sent = [join([pieces[s] for s in sources]) for mask, sources in steps[index : index + 2]]
        if index + 2 >= len(steps):
            sent[0], sent[1], item_feats = lax.optimization_barrier((sent[0], sent[1], item_feats))
        sent = [links.swap(v, m) for v, (m, _) in zip(sent, steps[index : index + 2])]
        if index + 2 >= len(steps):
            hidden_t, tower_out, vectors = tower(item_feats, first_t, second_t)
            sent[0], sent[1], hidden_t, tower_out, vectors = lax.optimization_barrier(
                (sent[0], sent[1], hidden_t, tower_out, vectors)
            )
        pieces += sent
    other = [links.swap(piece, core) for piece in pieces]
    all_pieces = pieces + other

    max_chunks = (slots + (SUB - 1) * own_blocks) // SUB + UNROLL + 1
    max_chunks += -max_chunks % 8
    spots = max_chunks * SUB
    tile_blocks = TILE // BLK
    n_tiles = item_rows // TILE
    column = me * capacity
    n_pieces = len(all_pieces)
    packed_rows = all_users // BLK
    i32 = functools.partial(jax.ShapeDtypeStruct, dtype=I32)
    sizes = (spots, n_tiles)
    plan, positions = pl.pallas_call(
        functools.partial(plan_kernel, n_pieces, capacity, tile_blocks, sizes),
        out_shape=(i32((Plan(None, *sizes).size,)), i32((packed_rows, BLK))),
        in_specs=[smem_spec()] * 2 + [any_spec()] * n_pieces,
        out_specs=(smem_spec(), vmem_spec()),
        scratch_shapes=[
            pltpu.VMEM((devices * HEAD, emb), BF16),
            pltpu.VMEM((devices * HEAD, BLK), F32),
            pltpu.VMEM((devices * HEAD, BLK), F32),
            pltpu.VMEM((2 * devices, BLK), I32),
            pltpu.SMEM((2 * devices, BLK), I32),
            pltpu.SMEM((own_blocks + 1,), I32),
            pltpu.SMEM((own_blocks + 1,), I32),
            pltpu.SemaphoreType.DMA((devices,)),
        ],
        name="plan",
        cost_estimate=busy(6),
    )(jnp.stack([column % BLK, me, column // BLK]), jnp.asarray(np.array(order), I32), *all_pieces)
    exp_scores, local, totals, pos_part = pl.pallas_call(
        functools.partial(score_kernel, n_pieces, group, sizes),
        out_shape=(
            jax.ShapeDtypeStruct((max_chunks * BLK, BLK), F32),
            jax.ShapeDtypeStruct((max_chunks, BLK), I32),
            jax.ShapeDtypeStruct((packed_rows, BLK), F32),
            jax.ShapeDtypeStruct((packed_rows, BLK), F32),
        ),
        grid_spec=pltpu.PrefetchScalarGridSpec(
            num_scalar_prefetch=1,
            grid=(1,),
            in_specs=[any_spec()] * n_pieces + [vmem_spec()] * 3,
            out_specs=[vmem_spec()] * 4,
            scratch_shapes=[
                pltpu.VMEM((all_users, emb), BF16),
                pltpu.VMEM((lists, BLK), I32),
                pltpu.VMEM((lists, BLK), F32),
                pltpu.VMEM((lists, BLK), F32),
                pltpu.SemaphoreType.DMA((devices,)),
            ],
        ),
        compiler_params=limit(60),
        name="scores",
        cost_estimate=busy(9),
    )(plan, *all_pieces, vectors, logs, positions)

    for bit in [links.core] + links.x + links.y + links.z[::-1]:
        totals = totals + links.swap(totals, 1 << bit)

    width = emb if all_users <= 8192 else BLK
    half_users = all_users // 2
    keeps, sends = [], []
    for low in range(0, emb, width):
        kept, sent, score_grad = pl.pallas_call(
            functools.partial(vector_kernel, group, LOSS_SCALE / all_users, (low, low + width), sizes),
            out_shape=(
                jax.ShapeDtypeStruct((half_users, width), F32),
                jax.ShapeDtypeStruct((half_users, width), BF16),
                jax.ShapeDtypeStruct((max_chunks * BLK, BLK), BF16),
            ),
            grid_spec=pltpu.PrefetchScalarGridSpec(
                num_scalar_prefetch=1,
                grid=(1,),
                in_specs=[vmem_spec()] * 4,
                out_specs=[any_spec(), vmem_spec(), vmem_spec()],
                scratch_shapes=[
                    pltpu.VMEM((lists, BLK), F32),
                    pltpu.VMEM((all_users, width), F32),
                    pltpu.SemaphoreType.DMA,
                ],
            ),
            compiler_params=limit(60),
            name="vector_grads",
            cost_estimate=busy(12),
        )(plan, vectors, exp_scores, local, totals)
        keeps.append(kept)
        sends.append(sent)
    keep = keeps[0] if len(keeps) == 1 else jnp.concatenate(keeps, axis=1)
    send = sends[0] if len(sends) == 1 else jnp.concatenate(sends, axis=1)

    out_gradient = pl.pallas_call(
        functools.partial(item_kernel, n_pieces, group, tile_blocks, sizes),
        out_shape=jax.ShapeDtypeStruct((item_rows, emb), BF16),
        grid_spec=pltpu.PrefetchScalarGridSpec(
            num_scalar_prefetch=1,
            grid=(n_tiles,),
            in_specs=[any_spec()] * n_pieces
            + [pl.BlockSpec((TILE, emb), lambda t, *_: (t, 0)), vmem_spec()],
            out_specs=pl.BlockSpec((TILE, emb), lambda t, *_: (t, 0)),
            scratch_shapes=[
                pltpu.VMEM((all_users, emb), BF16),
                pltpu.VMEM((TILE + BLK, emb), F32),
                pltpu.SemaphoreType.DMA((devices,)),
            ],
        ),
        compiler_params=limit(60),
        name="item_grads",
        cost_estimate=busy(10),
    )(plan, *all_pieces, tower_out, score_grad)

    small_bits = [links.core] + links.x + links.y + links.z[::-1]
    small = iter(small_bits)

    def pos_stage(pos):
        bit = next(small, None)
        return pos if bit is None else pos + links.swap(pos, 1 << bit)

    arrived = links.swap(send, core)
    pos_part = pos_stage(pos_part)
    arrived, pos_part, out_gradient = lax.optimization_barrier((arrived, pos_part, out_gradient))
    partial, offset = [], 0
    for piece in masks:
        rows = slice(offset, offset + len(piece) * user_rows)
        partial.append(LOGIT_SCALE * keep[rows] + arrived[rows].astype(F32))
        offset = rows.stop
    outgoing = [partial[-1].astype(BF16), partial[-2].astype(BF16)]
    outgoing[0], outgoing[1], out_gradient = lax.optimization_barrier(
        (outgoing[0], outgoing[1], out_gradient)
    )

    def receive(partial, index, outgoing=None):
        if outgoing is None:
            outgoing = partial[index + 1].astype(BF16)
        return links.swap(outgoing, steps[index][0])

    def back(partial, index, arrived):
        offset = 0
        partial = list(partial)
        for s in steps[index][1]:
            rows = partial[s].shape[0]
            partial[s] = partial[s] + arrived[offset : offset + rows].astype(F32)
            offset += rows
        return partial

    feat, hid = first_weight.shape
    first_gradient, second_gradient = pl.pallas_call(
        weight_kernel,
        out_shape=(
            jax.ShapeDtypeStruct((feat, hid), F32),
            jax.ShapeDtypeStruct((hid, emb), F32),
        ),
        grid=(n_tiles,),
        in_specs=[
            pl.BlockSpec((TILE, feat), lambda t: (t, 0)),
            pl.BlockSpec((hid, TILE), lambda t: (0, t)),
            vmem_spec(),
            pl.BlockSpec((TILE, emb), lambda t: (t, 0)),
        ],
        out_specs=[vmem_spec(), vmem_spec()],
        scratch_shapes=[pltpu.VMEM((hid, feat), F32)],
        compiler_params=limit(60),
        name="weight_grads",
        cost_estimate=busy(13),
    )(item_feats, hidden_t, second_weight, out_gradient)
    fold = hid // emb
    tall = hid // fold
    packed = jnp.concatenate(
        [first_gradient]
        + [jnp.concatenate([second_gradient[i * tall : (i + 1) * tall] for i in range(fold)], axis=1)],
        axis=0,
    )
    index = len(steps) - 1
    arrived = [receive(partial, index, outgoing[0]), receive(partial, index - 1, outgoing[1])]
    arrived[0], arrived[1], packed = lax.optimization_barrier((arrived[0], arrived[1], packed))
    partial = back(back(partial, index, arrived[0]), index - 1, arrived[1])
    index -= 2
    weights = WeightSum(links, me, packed)
    state = weights.core_stage()
    pos_part = pos_stage(pos_part)
    while index > n_z:
        if index == n_z + 1:
            state = weights.plane_stage(state)
        arrived = [receive(partial, index), receive(partial, index - 1)]
        pos_part = pos_stage(pos_part)
        arrived[0], arrived[1], pos_part, state = lax.optimization_barrier(
            (arrived[0], arrived[1], pos_part, state)
        )
        partial = back(back(partial, index, arrived[0]), index - 1, arrived[1])
        index -= 2
    for stage in (weights.line_sum, weights.line_spread):
        state = stage(state)
        arrived = receive(partial, index)
        pos_part = pos_stage(pos_part)
        arrived, pos_part, state = lax.optimization_barrier((arrived, pos_part, state))
        partial = back(partial, index, arrived)
        index -= 1
    total = weights.spread_stage(state)
    for bit in small:
        pos_part = pos_part + links.swap(pos_part, 1 << bit)

    own_rows = user_rows // BLK
    own_totals = lax.dynamic_slice(totals, (me * own_rows, 0), (own_rows, BLK))
    own_pos = lax.dynamic_slice(pos_part, (me * own_rows, 0), (own_rows, BLK))
    user_loss = (jnp.log(own_totals) - own_pos).reshape(user_rows)
    vector_grad = partial[0]
    user_projection = jnp.sum(user_float * vector_grad, axis=1, keepdims=True)
    user_gradient = vector_grad * user_norm - user_float * (
        user_projection * user_norm * user_norm * user_norm
    )
    first_total = total[:feat].astype(F32)
    second_total = jnp.concatenate(
        [total[feat:, i * emb : (i + 1) * emb] for i in range(fold)], axis=0
    ).astype(F32)
    return (user_loss, user_gradient, first_total, second_total)


def tower(item_feats, first_t, second_t):
    rows, feat = item_feats.shape
    emb, hid = second_t.shape
    return pl.pallas_call(
        tower_kernel,
        out_shape=(
            jax.ShapeDtypeStruct((hid, rows), BF16),
            jax.ShapeDtypeStruct((rows, emb), F32),
            jax.ShapeDtypeStruct((rows, emb), BF16),
        ),
        grid=(rows // TILE,),
        in_specs=[
            pl.BlockSpec((TILE, feat), lambda t: (t, 0)),
            vmem_spec(),
            vmem_spec(),
        ],
        out_specs=[
            pl.BlockSpec((hid, TILE), lambda t: (0, t)),
            pl.BlockSpec((TILE, emb), lambda t: (t, 0)),
            pl.BlockSpec((TILE, emb), lambda t: (t, 0)),
        ],
        compiler_params=limit(60),
        name="tower",
        cost_estimate=busy(11),
    )(item_feats, first_t, second_t)


class WeightSum:
    def __init__(self, links, me, value):
        self.links = links
        self.value = value
        self.half = value.shape[0] // 2
        self.core_bit = (me >> links.core) & 1
        self.plane = links.x + links.y
        self.ways = 1 << len(self.plane)
        self.part = self.half // self.ways
        self.place = (me >> links.z[1]) & 3
        self.own = sum(((me >> bit) & 1) << i for i, bit in enumerate(self.plane))

    def mask_of(self, way):
        return sum(1 << bit for i, bit in enumerate(self.plane) if (way >> i) & 1)

    def core_stage(self):
        half = self.half
        send = lax.dynamic_slice_in_dim(self.value, (1 - self.core_bit) * half, half, 0)
        mine = lax.dynamic_slice_in_dim(self.value, self.core_bit * half, half, 0)
        return mine + self.links.swap(send, 1 << self.links.core)

    def plane_stage(self, mine):
        arrived = []
        for way in range(1, self.ways):
            out = lax.dynamic_slice_in_dim(mine, (self.own ^ way) * self.part, self.part, 0)
            arrived.append(self.links.swap(out.astype(BF16), self.mask_of(way)))
        own_sum = lax.dynamic_slice_in_dim(mine, self.own * self.part, self.part, 0)
        for item in arrived:
            own_sum = own_sum + item.astype(F32)
        return own_sum

    def line_masks(self):
        low, high = self.links.z[1], self.links.z[0]
        return [1 << low, 1 << high, (1 << low) | (1 << high)]

    def line_sum(self, own_sum):
        rows = own_sum.shape[0] // 4
        arrived = []
        for way, mask in enumerate(self.line_masks(), 1):
            out = lax.dynamic_slice_in_dim(own_sum, (self.place ^ way) * rows, rows, 0)
            arrived.append(self.links.swap(out.astype(BF16), mask))
        total = lax.dynamic_slice_in_dim(own_sum, self.place * rows, rows, 0)
        for item in arrived:
            total = total + item.astype(F32)
        return total.astype(BF16)

    def line_spread(self, final):
        parts = [final] + [self.links.swap(final, mask) for mask in self.line_masks()]
        return self.arrange(parts, self.place)

    def arrange(self, parts, own):
        ways = len(parts)
        for i in range(ways.bit_length() - 1):
            bit = (own >> i) & 1
            step = 1 << i
            parts = [jnp.where(bit == 1, parts[q ^ step], parts[q]) for q in range(ways)]
        return jnp.concatenate(parts, axis=0)

    def spread_stage(self, final):
        ways = self.ways
        parts = [final] + [self.links.swap(final, self.mask_of(way)) for way in range(1, ways)]
        near = self.arrange(parts, self.own)
        far = self.links.swap(near, 1 << self.links.core)
        first = self.core_bit == 0
        return jnp.concatenate([jnp.where(first, near, far), jnp.where(first, far, near)], axis=0)


def solution(mesh):
    return jax.shard_map(
        body,
        mesh=mesh,
        in_specs=(
            P(("user", "item"), None),
            P(),
            P(),
            P(("user", "item")),
            P(("user", "item"), None),
            P(("user", "item"), None),
            P(("user", "item")),
            P(("user", "item")),
        ),
        out_specs=(P(("user", "item")), P(("user", "item"), None), P(), P()),
        check_vma=False,
    )
```

time: 277 us -> 214 us (0.77)
  waiting for transfers between devices: 106 us -> 51.3 us
  Pallas kernels: 37 us -> 73.1 us
  matrix products: 24.3 us -> 0 us
  other arithmetic: 43.3 us -> 26.1 us
  local copies, waits for them, and re-layouts: 22.2 us -> 10.2 us
  starting transfers between devices: 41.9 us -> 52.4 us
    ppermute x40 -> x45, waiting for transfers between devices: 106 us -> 51.3 us  [swap(): return lax.ppermute(value, AXES, pairs)]
    pallas_call x2 -> x6, Pallas kernels: 37 us -> 73.1 us  [the longest x1 13.5 us: body(): pl.pallas_call(weight_kernel, out_shape=(jax.ShapeDtypeStruct((feat, hid)...]
    dot_general x4 -> x0, matrix products: 24.3 us -> none  [the longest x1 11.6 us: body(): jnp.dot(item_feats.T, act_gradient, preferred_element_type=F32)]
    ppermute x40 -> x45, starting transfers between devices: 41.9 us -> 52.4 us  [swap(): return lax.ppermute(value, AXES, pairs)]
    reduce_sum x8 -> x0, other arithmetic: 6.39 us -> none  [the longest x1 4.22 us: body(): projection = jnp.sum(tower_out * item_gradient, axis=1, keepdims=True)]
    convert_element_type x13 -> x5, other arithmetic: 13.8 us -> 7.41 us  [the longest x3 3.85 us: receive(): outgoing = partial[index + 1].astype(BF16)]
    dot_general x1 -> x0, local copies, waits for them, and re-layouts: 5.6 us -> none  [body(): tower_out = jnp.dot(hidden, second_weight, preferred_element_type=F32)]
    another operation x1 -> x4, other arithmetic: 5.35 us -> 1.34 us
  transfers between devices with their start and end apart: 40 -> 45, of which waited for: 25 -> 22; matrix products, arithmetic and copies ran while one was open for 20% -> 10% of each run, Pallas kernels for 0% -> 18%
where the time goes in v2:
time: 214 us
  Pallas kernels  73.1 us (34%)
  starting transfers between devices  52.4 us (24%)
  waiting for transfers between devices  51.3 us (24%)
  other arithmetic  26.1 us (12%)
  local copies, waits for them, and re-layouts  10.2 us (5%)
    ppermute x45, starting transfers between devices, swap(): return lax.ppermute(value, AXES, pairs)  52.4 us
    ppermute x45, waiting for transfers between devices, swap(): return lax.ppermute(value, AXES, pairs)  51.3 us
    pallas_call x1, Pallas kernels, body(): pl.pallas_call(weight_kernel, out_shape=(jax.ShapeDtypeStruct((feat, hid)...  13.5 us
    pallas_call x1, Pallas kernels, body(): pl.pallas_call(functools.partial(vector_kernel, group, LOSS_SCALE / all_u...  13.2 us
    pallas_call x1, Pallas kernels, body(): pl.pallas_call(functools.partial(item_kernel, n_pieces, group, tile_block...  13.2 us
    pallas_call x1, Pallas kernels, tower(): pl.pallas_call(tower_kernel, out_shape=(jax.ShapeDtypeStruct((hid, rows),...  12.7 us
    pallas_call x1, Pallas kernels, body(): pl.pallas_call(functools.partial(score_kernel, n_pieces, group, sizes), o...  11.6 us
    pallas_call x1, Pallas kernels, body(): pl.pallas_call(functools.partial(plan_kernel, n_pieces, capacity, tile_bl...  8.8 us
  transfers between devices with their start and end apart: 45, of which 22 were waited for; matrix products, arithmetic and copies ran while one was open for 10% of the time, Pallas kernels for 18%

profile of v2, /device:TPU:0, one launch (start us, length us, event | category | flops | bytes accessed | tf_op | source)
XLA Modules:
  0.0 214.2 jit_solution(5351052326336068193)
XLA Ops:
  0.6 1.1 fusion.1
  1.7 1.0 constant_dynamic-update-slice_fusion.6
  2.7 4.1 %collective-permute-start = (bf16[256,256]{1,0:T(8,128)(2,1)S(1)}, bf16[256,256]{1,0:T(8,128)(2,1)S(1)}, u32[]{:S(2)}, u32[]{:S(2)}) collective-permute-start(bf16[256,256]{1,0:T(8,128)(2,1)S(1)} %get-tuple-element.99), channel_id=1, source_target_pairs={{0,4},{1,5},{2,6},{3,7},{4,0},{5,1},{6,2},{7,3},{8,12},{9,13},{10,... | collective-permute-start | bytes 393224 | tf_op jit(solution)/shard_map/ppermute | solution.py:43
  10.8 2.3 %copy.15 = bf16[1024,512]{0,1:T(8,128)(2,1)} copy(bf16[1024,512]{1,0:T(8,128)(2,1)} %param.10) | data formatting | bytes 2097152 | tf_op args[1]
  13.9 1.9 broadcast_in_dim.35.refs_15_
  15.8 2.0 collective-permute-start.2
  17.8 1.5 collective-permute-start.3
  19.3 4.7 %collective-permute-done.2.refs_2_ = bf16[544,256]{1,0:T(8,128)(2,1)S(1)} collective-permute-done((bf16[544,256]{1,0:T(8,128)(2,1)S(1)}, bf16[544,256]{1,0:T(8,128)(2,1)S(1)}, u32[]{:S(2)}, u32[]{:S(2)}) %collective-permute-start.2) | collective-permute-done | bytes 278560 | tf_op jit(solution)/shard_map/ppermute | solution.py:43
  24.0 1.5 collective-permute-start.4
  25.6 5.6 %collective-permute-done.4.refs_4_ = bf16[544,256]{1,0:T(8,128)(2,1)S(1)} collective-permute-done((bf16[544,256]{1,0:T(8,128)(2,1)S(1)}, bf16[544,256]{1,0:T(8,128)(2,1)S(1)}, u32[]{:S(2)}, u32[]{:S(2)}) %collective-permute-start.4) | collective-permute-done | bytes 278560 | tf_op jit(solution)/shard_map/ppermute | solution.py:43
  31.3 1.3 collective-permute-start.5
  32.6 1.5 collective-permute-start.6
  34.1 12.7 %tower.1 = (bf16[512,4096]{1,0:T(8,128)(2,1)}, f32[4096,256]{1,0:T(8,128)}, bf16[4096,256]{1,0:T(8,128)(2,1)}) custom-call(bf16[4096,1024]{1,0:T(8,128)(2,1)} %feats.1, bf16[512,1024]{1,0:T(8,128)(2,1)} %bitcast.14, bf16[256,512]{1,0:T(8,128)(2,1)} %bitcast.15), custom_call_target="tpu_custom_call" | custom-call | flops 11000000512 | bytes 33000000 | tf_op jit(solution)/shard_map/tower/pallas_call | solution.py:685
  48.0 1.2 collective-permute-done.7.refs_7_
  52.1 8.8 %plan.1 = (s32[874]{0:T(1024)}, s32[64,128]{1,0:T(8,128)}) custom-call(s32[3]{0:T(128)} %pad_add_fusion.where, s32[32]{0:T(128)} %constant.85.clone.masks, bf16[272,256]{1,0:T(8,128)(2,1)} %copy-done.10, bf16[272,256]{1,0:T(8,128)(2,1)} %copy-done.11, bf16[544,256]{1,0:T(8,128)(2,1)} %copy-done.6, bf16[544,256]{1,0:T(8,128)(2,1)} %copy-done.7, ...), custom_call_target="tpu_custom_call" | custom-call | flops 6000000000 | bytes 18000000 | tf_op jit(solution)/shard_map/plan/pallas_call | solution.py:478
  60.9 11.6 %scores.1 = (f32[12288,128]{1,0:T(8,128)}, s32[96,128]{1,0:T(8,128)}, f32[64,128]{1,0:T(8,128)}, f32[64,128]{1,0:T(8,128)}) custom-call(s32[874]{0:T(1024)} %get-tuple-element.60.plan_ref, bf16[272,256]{1,0:T(8,128)(2,1)} %copy-done.10, bf16[272,256]{1,0:T(8,128)(2,1)} %copy-done.11, bf16[544,256]{1,0:T(8,128)(2,1)} %copy-done.6, ...), custom_call_target="tpu_custom_call" | custom-call | flops 8999999488 | bytes 27000000 | tf_op jit(solution)/shard_map/scores/pallas_call | solution.py:496
  72.6 1.4 collective-permute-done.14
  75.4 3.3 %collective-permute-done.15 = f32[64,128]{1,0:T(8,128)S(1)} collective-permute-done((f32[64,128]{1,0:T(8,128)S(1)}, f32[64,128]{1,0:T(8,128)S(1)}, u32[]{:S(2)}, u32[]{:S(2)}) %collective-permute-start.15) | collective-permute-done | bytes 32800 | tf_op jit(solution)/shard_map/ppermute | solution.py:43
  79.3 3.4 %collective-permute-done.16 = f32[64,128]{1,0:T(8,128)S(1)} collective-permute-done((f32[64,128]{1,0:T(8,128)S(1)}, f32[64,128]{1,0:T(8,128)S(1)}, u32[]{:S(2)}, u32[]{:S(2)}) %collective-permute-start.16) | collective-permute-done | bytes 32800 | tf_op jit(solution)/shard_map/ppermute | solution.py:43
  82.6 1.3 collective-permute-start.17
  83.9 2.6 %collective-permute-done.17 = f32[64,128]{1,0:T(8,128)S(1)} collective-permute-done((f32[64,128]{1,0:T(8,128)S(1)}, f32[64,128]{1,0:T(8,128)S(1)}, u32[]{:S(2)}, u32[]{:S(2)}) %collective-permute-start.17) | collective-permute-done | bytes 32800 | tf_op jit(solution)/shard_map/ppermute | solution.py:43
  86.6 3.3 %collective-permute-start.18 = (f32[64,128]{1,0:T(8,128)S(1)}, f32[64,128]{1,0:T(8,128)S(1)}, u32[]{:S(2)}, u32[]{:S(2)}) collective-permute-start(f32[64,128]{1,0:T(8,128)S(1)} %add.199), channel_id=1, source_target_pairs={{0,4},{1,5},{2,6},{3,7},{4,0},{5,1},{6,2},{7,3},{8,12},{9,13},{10,... | collective-permute-start | bytes 98312 | tf_op jit(solution)/shard_map/ppermute | solution.py:43
  89.9 1.9 collective-permute-done.18
  92.4 13.2 %vector_grads.1 = (f32[4096,256]{1,0:T(8,128)}, bf16[4096,256]{1,0:T(8,128)(2,1)}, bf16[12288,128]{1,0:T(8,128)(2,1)}) custom-call(s32[874]{0:T(1024)} %get-tuple-element.60.plan_ref, bf16[4096,256]{1,0:T(8,128)(2,1)} %get-tuple-element.61.refs_14_.refs_0_, f32[12288,128]{1,0:T(8,128)} %get-tuple-element.65.refs_1_, s32[96,128]{1,0:T(8,128)} %get-tuple-element.66.refs_2_, ...), custom_call_target="tpu_custom_call" | custom-call | flops 12000000000 | bytes 36000000 | tf_op jit(solution)/shard_map/vector_grads/pallas_call | solution.py:529
  106.2 3.3 %collective-permute-done.20 = f32[64,128]{1,0:T(8,128)S(1)} collective-permute-done((f32[64,128]{1,0:T(8,128)S(1)}, f32[64,128]{1,0:T(8,128)S(1)}, u32[]{:S(2)}, u32[]{:S(2)}) %collective-permute-start.20) | collective-permute-done | bytes 32800 | tf_op jit(solution)/shard_map/ppermute | solution.py:43
  109.6 13.2 %item_grads.1.out_gradient = bf16[4096,256]{1,0:T(8,128)(2,1)} custom-call(s32[874]{0:T(1024)} %get-tuple-element.60.plan_ref, bf16[272,256]{1,0:T(8,128)(2,1)} %copy-done.10, bf16[272,256]{1,0:T(8,128)(2,1)} %copy-done.11, bf16[544,256]{1,0:T(8,128)(2,1)} %copy-done.6, bf16[544,256]{1,0:T(8,128)(2,1)} %copy-done.7, bf16[544,256]{1,0:T(8,128)(2,1)} %copy-done.8, ...), custom_call_target="tpu_custom_call" | custom-call | flops 10000000000 | bytes 30000000 | tf_op jit(solution)/shard_map/item_grads/pallas_call | solution.py:556
  122.8 3.5 %add_convert_fusion = (bf16[1024,256]{1,0:T(8,128)(2,1)}, bf16[1024,256]{1,0:T(8,128)(2,1)}) fusion(f32[4096,256]{1,0:T(8,128)} %get-tuple-element.67, bf16[4096,256]{1,0:T(8,128)(2,1)S(1)} %collective-permute-done.19), kind=kLoop, calls=%fused_computation.4 | loop fusion | flops 2097152 | bytes 4194304 | tf_op jit(solution)/shard_map/convert_element_type | solution.py:591
  126.3 2.1 collective-permute-start.21
  128.4 13.5 %weight_grads.1 = (f32[1024,512]{1,0:T(8,128)}, f32[512,256]{1,0:T(8,128)}) custom-call(bf16[4096,1024]{1,0:T(8,128)(2,1)} %feats.1, bf16[512,4096]{1,0:T(8,128)(2,1)} %get-tuple-element.76.hidden_t, bf16[512,256]{1,0:T(8,128)(2,1)} %second.1, bf16[4096,256]{1,0:T(8,128)(2,1)} %item_grads.1.out_gradient), custom_call_target="tpu_custom_call" | custom-call | flops 12999999488 | bytes 39000000 | tf_op jit(solution)/shard_map/weight_grads/pallas_call | solution.py:611
  142.0 1.1 fusion.22
  143.0 1.9 maximum_maximum_fusion
  145.7 1.2 constant_dynamic-slice_fusion.1
  147.0 1.9 collective-permute-start.25
  148.9 2.1 collective-permute-done.25
  151.3 1.6 dynamic-slice_add_fusion
  152.9 1.1 copy-done
  154.1 1.8 collective-permute-start.28
  155.8 1.9 collective-permute-start.29
  157.8 1.5 add_convert_fusion.3
  159.3 1.6 collective-permute-start.23
  160.9 1.9 collective-permute-start.24
  162.9 1.9 collective-permute-done.29
  164.8 1.0 collective-permute-done.30
  165.8 1.0 convert_add_fusion
  166.8 2.2 %collective-permute-done.23 = bf16[512,256]{1,0:T(8,128)(2,1)S(1)} collective-permute-done((bf16[512,256]{1,0:T(8,128)(2,1)S(1)}, bf16[512,256]{1,0:T(8,128)(2,1)S(1)}, u32[]{:S(2)}, u32[]{:S(2)}) %collective-permute-start.23) | collective-permute-done | bytes 262176 | tf_op jit(solution)/shard_map/ppermute | solution.py:43
  169.1 1.2 collective-permute-done.24
  170.5 6.1 %collective-permute-start.34 = (bf16[40,512]{1,0:T(8,128)(2,1)S(1)}, bf16[40,512]{1,0:T(8,128)(2,1)S(1)}, u32[]{:S(2)}, u32[]{:S(2)}) collective-permute-start(bf16[40,512]{1,0:T(8,128)(2,1)S(1)} %get-tuple-element.119), channel_id=1, source_target_pairs={{0,4},{1,5},{2,6},{3,7},{4,0},{5,1},{6,2},{7,3},{8,12},{9,13},{10,... | collective-permute-start | bytes 122888 | tf_op jit(solution)/shard_map/ppermute | solution.py:43
  176.6 1.4 collective-permute-start.35
  178.0 1.2 add_convert_fusion.2
  179.8 1.5 collective-permute-start.32
  181.3 6.3 %collective-permute-done.32 = f32[64,128]{1,0:T(8,128)S(1)} collective-permute-done((f32[64,128]{1,0:T(8,128)S(1)}, f32[64,128]{1,0:T(8,128)S(1)}, u32[]{:S(2)}, u32[]{:S(2)}) %collective-permute-start.32) | collective-permute-done | bytes 32800 | tf_op jit(solution)/shard_map/ppermute | solution.py:43
  187.7 2.5 %collective-permute-start.38 = (bf16[40,512]{1,0:T(8,128)(2,1)S(1)}, bf16[40,512]{1,0:T(8,128)(2,1)S(1)}, u32[]{:S(2)}, u32[]{:S(2)}) collective-permute-start(bf16[40,512]{1,0:T(8,128)(2,1)S(1)} %add_convert_fusion.6), channel_id=1, source_target_pairs={{0,6},{1,7},{2,4},{3,5},{4,2},{5,3},{6,0},{7,1},{8,14},{9,15},{10,... | collective-permute-start | bytes 122888 | tf_op jit(solution)/shard_map/ppermute | solution.py:43
  190.1 2.0 collective-permute-start.40
  193.1 1.1 add_convert_fusion.5
  194.1 2.1 collective-permute-start.36
  196.2 2.6 %collective-permute-done.37 = f32[64,128]{1,0:T(8,128)S(1)} collective-permute-done((f32[64,128]{1,0:T(8,128)S(1)}, f32[64,128]{1,0:T(8,128)S(1)}, u32[]{:S(2)}, u32[]{:S(2)}) %collective-permute-start.37) | collective-permute-done | bytes 32800 | tf_op jit(solution)/shard_map/ppermute | solution.py:43
  198.9 1.3 collective-permute-done.36
  200.2 1.7 collective-permute-start.41
  201.9 1.8 collective-permute-start.43
  203.7 1.2 fusion.16
  205.0 2.5 %collective-permute-done.41 = bf16[160,512]{1,0:T(8,128)(2,1)S(1)} collective-permute-done((bf16[160,512]{1,0:T(8,128)(2,1)S(1)}, bf16[160,512]{1,0:T(8,128)(2,1)S(1)}, u32[]{:S(2)}, u32[]{:S(2)}) %collective-permute-start.41) | collective-permute-done | bytes 163872 | tf_op jit(solution)/shard_map/ppermute | solution.py:43
  207.5 1.7 collective-permute-done.42
  209.4 1.2 fusion.3
  211.8 1.6 fusion
  (132 shorter events, 17.4 us)
Async XLA Ops:
  0.6 12.4 %copy-start.9 = (bf16[512,256]{1,0:T(8,128)(2,1)S(1)}, bf16[512,256]{1,0:T(8,128)(2,1)}, u32[]{:S(2)}) copy-start(bf16[512,256]{1,0:T(8,128)(2,1)} %second.1) | copy-start | bytes 786436
  2.7 11.2 %collective-permute-start = (bf16[256,256]{1,0:T(8,128)(2,1)S(1)}, bf16[256,256]{1,0:T(8,128)(2,1)S(1)}, u32[]{:S(2)}, u32[]{:S(2)}) collective-permute-start(bf16[256,256]{1,0:T(8,128)(2,1)S(1)} %get-tuple-element.99), channel_id=1, source_target_pairs={{0,4},{1,5},{2,6},{3,7},{4,0},{5,1},{6,2},{7,3},{8,12},{9,13},{10,... | collective-permute-start | bytes 393224 | tf_op jit(solution)/shard_map/ppermute | solution.py:43
  10.0 5.8 %collective-permute-start.1 = (bf16[16,256]{1,0:T(8,128)(2,1)S(1)}, bf16[16,256]{1,0:T(8,128)(2,1)S(1)}, u32[]{:S(2)}, u32[]{:S(2)}) collective-permute-start(bf16[16,256]{1,0:T(8,128)(2,1)S(1)} %get-tuple-element.129), channel_id=1, source_target_pairs={{0,4},{1,5},{2,6},{3,7},{4,0},{5,1},{6,2},{7,3},{8,12},{9,13},{10,... | collective-permute-start | bytes 24584 | tf_op jit(solution)/shard_map/ppermute | solution.py:43
  15.8 8.2 %collective-permute-start.2 = (bf16[544,256]{1,0:T(8,128)(2,1)S(1)}, bf16[544,256]{1,0:T(8,128)(2,1)S(1)}, u32[]{:S(2)}, u32[]{:S(2)}) collective-permute-start(bf16[544,256]{1,0:T(8,128)(2,1)S(1)} %pad_maximum_fusion.3), channel_id=1, source_target_pairs={{0,2},{1,3},{2,0},{3,1},{4,6},{5,7},{6,4},{7,5},{8,10},{9,11},{10,... | collective-permute-start | bytes 835592 | tf_op jit(solution)/shard_map/ppermute | solution.py:43
  17.8 7.8 %collective-permute-start.3 = (bf16[544,256]{1,0:T(8,128)(2,1)S(1)}, bf16[544,256]{1,0:T(8,128)(2,1)S(1)}, u32[]{:S(2)}, u32[]{:S(2)}) collective-permute-start(bf16[544,256]{1,0:T(8,128)(2,1)S(1)} %pad_maximum_fusion.3), channel_id=1, source_target_pairs={{0,1},{1,0},{2,3},{3,2},{4,5},{5,4},{6,7},{7,6},{8,9},{9,8},{10,11... | collective-permute-start | bytes 835592 | tf_op jit(solution)/shard_map/ppermute | solution.py:43
  24.0 23.9 %copy-start.6 = (bf16[544,256]{1,0:T(8,128)(2,1)}, bf16[544,256]{1,0:T(8,128)(2,1)S(1)}, u32[]{:S(2)}) copy-start(bf16[544,256]{1,0:T(8,128)(2,1)S(1)} %collective-permute-done.2.refs_2_) | copy-start | bytes 835588
  24.0 7.2 %collective-permute-start.4 = (bf16[544,256]{1,0:T(8,128)(2,1)S(1)}, bf16[544,256]{1,0:T(8,128)(2,1)S(1)}, u32[]{:S(2)}, u32[]{:S(2)}) collective-permute-start(bf16[544,256]{1,0:T(8,128)(2,1)S(1)} %collective-permute-done.2.refs_2_), channel_id=1, source_target_pairs={{0,16},{1,17},{2,18},{3,19},{4,20},{5,21},{6,22},{7,23},{8,24},{9,... | collective-permute-start | bytes 835592 | tf_op jit(solution)/shard_map/ppermute | solution.py:43
  25.6 21.9 %copy-start.11 = (bf16[272,256]{1,0:T(8,128)(2,1)}, bf16[272,256]{1,0:T(8,128)(2,1)S(1)}, u32[]{:S(2)}) copy-start(bf16[272,256]{1,0:T(8,128)(2,1)S(1)} %get-tuple-element.127.refs_1_) | copy-start | bytes 417796
  25.6 23.6 %copy-start.7 = (bf16[544,256]{1,0:T(8,128)(2,1)}, bf16[544,256]{1,0:T(8,128)(2,1)S(1)}, u32[]{:S(2)}) copy-start(bf16[544,256]{1,0:T(8,128)(2,1)S(1)} %collective-permute-done.3.refs_3_) | copy-start | bytes 835588
  31.2 18.4 %copy-start.8 = (bf16[544,256]{1,0:T(8,128)(2,1)}, bf16[544,256]{1,0:T(8,128)(2,1)S(1)}, u32[]{:S(2)}) copy-start(bf16[544,256]{1,0:T(8,128)(2,1)S(1)} %collective-permute-done.4.refs_4_) | copy-start | bytes 835588
  31.3 15.5 %collective-permute-start.5 = (bf16[1088,256]{1,0:T(8,128)(2,1)S(1)}, bf16[1088,256]{1,0:T(8,128)(2,1)S(1)}, u32[]{:S(2)}, u32[]{:S(2)}) collective-permute-start(bf16[1088,256]{1,0:T(8,128)(2,1)S(1)} %constant_dynamic-update-slice_fusion.2), channel_id=1, source_target_pairs={{0,16},{1,17},{2,18},{3,19},{4,20},{5,21},{6,22},{7,23},{8,24},{9,... | collective-permute-start | bytes 1671176 | tf_op jit(solution)/shard_map/ppermute | solution.py:43
  32.6 14.2 %collective-permute-start.6 = (bf16[1088,256]{1,0:T(8,128)(2,1)S(1)}, bf16[1088,256]{1,0:T(8,128)(2,1)}, u32[]{:S(2)}, u32[]{:S(2)}) collective-permute-start(bf16[1088,256]{1,0:T(8,128)(2,1)S(1)} %pad_maximum_fusion.2), channel_id=1, source_target_pairs={{0,1},{1,0},{2,3},{3,2},{4,5},{5,4},{6,7},{7,6},{8,9},{9,8},{10,11... | collective-permute-start | bytes 1671176 | tf_op jit(solution)/shard_map/ppermute | solution.py:43
  46.8 4.4 %copy-start.13 = (bf16[1088,256]{1,0:T(8,128)(2,1)}, bf16[1088,256]{1,0:T(8,128)(2,1)S(1)}, u32[]{:S(2)}) copy-start(bf16[1088,256]{1,0:T(8,128)(2,1)S(1)} %collective-permute-done.5.refs_5_) | copy-start | bytes 1671172
  46.8 4.4 %collective-permute-start.12 = (bf16[1088,256]{1,0:T(8,128)(2,1)S(1)}, bf16[1088,256]{1,0:T(8,128)(2,1)S(1)}, u32[]{:S(2)}, u32[]{:S(2)}) collective-permute-start(bf16[1088,256]{1,0:T(8,128)(2,1)S(1)} %collective-permute-done.5.refs_5_), channel_id=1, source_target_pairs={{0,8},{1,9},{2,10},{3,11},{4,12},{5,13},{6,14},{7,15},{8,0},{9,1},... | collective-permute-start | bytes 1671176 | tf_op jit(solution)/shard_map/ppermute | solution.py:43
  46.9 4.3 %collective-permute-start.13 = (bf16[1088,256]{1,0:T(8,128)(2,1)}, bf16[1088,256]{1,0:T(8,128)(2,1)}, u32[]{:S(2)}, u32[]{:S(2)}) collective-permute-start(bf16[1088,256]{1,0:T(8,128)(2,1)} %collective-permute-done.6.refs_6_), channel_id=1, source_target_pairs={{0,8},{1,9},{2,10},{3,11},{4,12},{5,13},{6,14},{7,15},{8,0},{9,1},... | collective-permute-start | bytes 1671176 | tf_op jit(solution)/shard_map/ppermute | solution.py:43
  47.4 3.8 %copy-start.10 = (bf16[272,256]{1,0:T(8,128)(2,1)}, bf16[272,256]{1,0:T(8,128)(2,1)S(1)}, u32[]{:S(2)}) copy-start(bf16[272,256]{1,0:T(8,128)(2,1)S(1)} %pad_maximum_fusion.5.refs_0_) | copy-start | bytes 417796
  47.4 1.8 collective-permute-start.7
  47.5 2.1 collective-permute-start.8
  48.0 2.5 %collective-permute-start.9 = (bf16[544,256]{1,0:T(8,128)(2,1)S(1)}, bf16[544,256]{1,0:T(8,128)(2,1)S(1)}, u32[]{:S(2)}, u32[]{:S(2)}) collective-permute-start(bf16[544,256]{1,0:T(8,128)(2,1)S(1)} %collective-permute-done.2.refs_2_), channel_id=1, source_target_pairs={{0,8},{1,9},{2,10},{3,11},{4,12},{5,13},{6,14},{7,15},{8,0},{9,1},... | collective-permute-start | bytes 835592 | tf_op jit(solution)/shard_map/ppermute | solution.py:43
  49.2 2.0 copy-start.18
  49.2 1.6 collective-permute-start.10
  49.6 1.6 copy-start.19
  49.6 1.6 collective-permute-start.11
  50.4 0.8 copy-start.15
  51.2 0.7 copy-start.17
  51.2 0.9 copy-start.14
  72.5 1.5 collective-permute-start.14
  74.8 3.9 %collective-permute-start.15 = (f32[64,128]{1,0:T(8,128)S(1)}, f32[64,128]{1,0:T(8,128)S(1)}, u32[]{:S(2)}, u32[]{:S(2)}) collective-permute-start(f32[64,128]{1,0:T(8,128)S(1)} %add.196), channel_id=1, source_target_pairs={{0,16},{1,17},{2,18},{3,19},{4,20},{5,21},{6,22},{7,23},{8,24},{9,... | collective-permute-start | bytes 98312 | tf_op jit(solution)/shard_map/ppermute | solution.py:43
  78.7 3.9 %collective-permute-start.16 = (f32[64,128]{1,0:T(8,128)S(1)}, f32[64,128]{1,0:T(8,128)S(1)}, u32[]{:S(2)}, u32[]{:S(2)}) collective-permute-start(f32[64,128]{1,0:T(8,128)S(1)} %add.197), channel_id=1, source_target_pairs={{0,1},{1,0},{2,3},{3,2},{4,5},{5,4},{6,7},{7,6},{8,9},{9,8},{10,11... | collective-permute-start | bytes 98312 | tf_op jit(solution)/shard_map/ppermute | solution.py:43
  82.6 3.9 %collective-permute-start.17 = (f32[64,128]{1,0:T(8,128)S(1)}, f32[64,128]{1,0:T(8,128)S(1)}, u32[]{:S(2)}, u32[]{:S(2)}) collective-permute-start(f32[64,128]{1,0:T(8,128)S(1)} %add.198), channel_id=1, source_target_pairs={{0,2},{1,3},{2,0},{3,1},{4,6},{5,7},{6,4},{7,5},{8,10},{9,11},{10,... | collective-permute-start | bytes 98312 | tf_op jit(solution)/shard_map/ppermute | solution.py:43
  86.6 5.3 %collective-permute-start.18 = (f32[64,128]{1,0:T(8,128)S(1)}, f32[64,128]{1,0:T(8,128)S(1)}, u32[]{:S(2)}, u32[]{:S(2)}) collective-permute-start(f32[64,128]{1,0:T(8,128)S(1)} %add.199), channel_id=1, source_target_pairs={{0,4},{1,5},{2,6},{3,7},{4,0},{5,1},{6,2},{7,3},{8,12},{9,13},{10,... | collective-permute-start | bytes 98312 | tf_op jit(solution)/shard_map/ppermute | solution.py:43
  92.4 13.3 %copy-start.12 = (f32[64,128]{1,0:T(8,128)S(1)}, f32[64,128]{1,0:T(8,128)}, u32[]{:S(2)}) copy-start(f32[64,128]{1,0:T(8,128)} %get-tuple-element.69) | copy-start | bytes 98308
  105.7 17.1 %collective-permute-start.19 = (bf16[4096,256]{1,0:T(8,128)(2,1)}, bf16[4096,256]{1,0:T(8,128)(2,1)S(1)}, u32[]{:S(2)}, u32[]{:S(2)}) collective-permute-start(bf16[4096,256]{1,0:T(8,128)(2,1)} %get-tuple-element.68), channel_id=1, source_target_pairs={{0,8},{1,9},{2,10},{3,11},{4,12},{5,13},{6,14},{7,15},{8,0},{9,1},... | collective-permute-start | bytes 6291464 | tf_op jit(solution)/shard_map/ppermute | solution.py:43
  105.7 3.8 %collective-permute-start.20 = (f32[64,128]{1,0:T(8,128)S(1)}, f32[64,128]{1,0:T(8,128)S(1)}, u32[]{:S(2)}, u32[]{:S(2)}) collective-permute-start(f32[64,128]{1,0:T(8,128)S(1)} %copy-done.12), channel_id=1, source_target_pairs={{0,8},{1,9},{2,10},{3,11},{4,12},{5,13},{6,14},{7,15},{8,0},{9,1},... | collective-permute-start | bytes 98312 | tf_op jit(solution)/shard_map/ppermute | solution.py:43
  122.8 3.5 %copy-start.2 = (bf16[4096,256]{1,0:T(8,128)(2,1)}, bf16[4096,256]{1,0:T(8,128)(2,1)S(1)}, u32[]{:S(2)}) copy-start(bf16[4096,256]{1,0:T(8,128)(2,1)S(1)} %collective-permute-done.19) | copy-start | bytes 6291460
  126.3 18.6 %collective-permute-start.21 = (bf16[1024,256]{1,0:T(8,128)(2,1)}, bf16[1024,256]{1,0:T(8,128)(2,1)S(1)}, u32[]{:S(2)}, u32[]{:S(2)}) collective-permute-start(bf16[1024,256]{1,0:T(8,128)(2,1)} %get-tuple-element.74), channel_id=1, source_target_pairs={{0,1},{1,0},{2,3},{3,2},{4,5},{5,4},{6,7},{7,6},{8,9},{9,8},{10,11... | collective-permute-start | bytes 1572872 | tf_op jit(solution)/shard_map/ppermute | solution.py:43
  128.4 16.5 %collective-permute-start.22 = (bf16[1024,256]{1,0:T(8,128)(2,1)}, bf16[1024,256]{1,0:T(8,128)(2,1)S(1)}, u32[]{:S(2)}, u32[]{:S(2)}) collective-permute-start(bf16[1024,256]{1,0:T(8,128)(2,1)} %get-tuple-element.75), channel_id=1, source_target_pairs={{0,16},{1,17},{2,18},{3,19},{4,20},{5,21},{6,22},{7,23},{8,24},{9,... | collective-permute-start | bytes 1572872 | tf_op jit(solution)/shard_map/ppermute | solution.py:43
  144.9 0.8 copy-start.3
  146.9 4.4 %collective-permute-start.27 = (f32[640,512]{1,0:T(8,128)}, f32[640,512]{1,0:T(8,128)}, u32[]{:S(2)}, u32[]{:S(2)}) collective-permute-start(f32[640,512]{1,0:T(8,128)} %constant_dynamic-slice_fusion.1), channel_id=1, source_target_pairs={{0,8},{1,9},{2,10},{3,11},{4,12},{5,13},{6,14},{7,15},{8,0},{9,1},... | collective-permute-start | bytes 3932168 | tf_op jit(solution)/shard_map/ppermute | solution.py:43
  147.0 4.0 %collective-permute-start.25 = (f32[64,128]{1,0:T(8,128)S(1)}, f32[64,128]{1,0:T(8,128)S(1)}, u32[]{:S(2)}, u32[]{:S(2)}) collective-permute-start(f32[64,128]{1,0:T(8,128)S(1)} %add.202), channel_id=1, source_target_pairs={{0,16},{1,17},{2,18},{3,19},{4,20},{5,21},{6,22},{7,23},{8,24},{9,... | collective-permute-start | bytes 98312 | tf_op jit(solution)/shard_map/ppermute | solution.py:43
  151.0 6.8 %copy-start.4 = (bf16[1024,256]{1,0:T(8,128)(2,1)S(1)}, bf16[1024,256]{1,0:T(8,128)(2,1)}, u32[]{:S(2)}) copy-start(bf16[1024,256]{1,0:T(8,128)(2,1)} %copy-done.3) | copy-start | bytes 1572868
  151.0 9.9 %collective-permute-start.26 = (f32[64,128]{1,0:T(8,128)S(1)}, f32[64,128]{1,0:T(8,128)S(1)}, u32[]{:S(2)}, u32[]{:S(2)}) collective-permute-start(f32[64,128]{1,0:T(8,128)S(1)} %add.211), channel_id=1, source_target_pairs={{0,1},{1,0},{2,3},{3,2},{4,5},{5,4},{6,7},{7,6},{8,9},{9,8},{10,11... | collective-permute-start | bytes 98312 | tf_op jit(solution)/shard_map/ppermute | solution.py:43
  152.9 1.1 copy-start
  154.0 23.9 %copy-start.5 = (bf16[1024,256]{1,0:T(8,128)(2,1)S(1)}, bf16[1024,256]{1,0:T(8,128)(2,1)}, u32[]{:S(2)}) copy-start(bf16[1024,256]{1,0:T(8,128)(2,1)} %copy-done.3) | copy-start | bytes 1572868
  154.1 8.8 %collective-permute-start.28 = (bf16[160,512]{1,0:T(8,128)(2,1)S(1)}, bf16[160,512]{1,0:T(8,128)(2,1)S(1)}, u32[]{:S(2)}, u32[]{:S(2)}) collective-permute-start(bf16[160,512]{1,0:T(8,128)(2,1)S(1)} %get-tuple-element.106), channel_id=1, source_target_pairs={{0,16},{1,17},{2,18},{3,19},{4,20},{5,21},{6,22},{7,23},{8,24},{9,... | collective-permute-start | bytes 491528 | tf_op jit(solution)/shard_map/ppermute | solution.py:43
  155.8 9.0 %collective-permute-start.29 = (bf16[160,512]{1,0:T(8,128)(2,1)S(1)}, bf16[160,512]{1,0:T(8,128)(2,1)S(1)}, u32[]{:S(2)}, u32[]{:S(2)}) collective-permute-start(bf16[160,512]{1,0:T(8,128)(2,1)S(1)} %get-tuple-element.108), channel_id=1, source_target_pairs={{0,1},{1,0},{2,3},{3,2},{4,5},{5,4},{6,7},{7,6},{8,9},{9,8},{10,11... | collective-permute-start | bytes 491528 | tf_op jit(solution)/shard_map/ppermute | solution.py:43
  157.8 8.0 %collective-permute-start.30 = (bf16[160,512]{1,0:T(8,128)(2,1)S(1)}, bf16[160,512]{1,0:T(8,128)(2,1)S(1)}, u32[]{:S(2)}, u32[]{:S(2)}) collective-permute-start(bf16[160,512]{1,0:T(8,128)(2,1)S(1)} %get-tuple-element.107), channel_id=1, source_target_pairs={{0,17},{1,16},{2,19},{3,18},{4,21},{5,20},{6,23},{7,22},{8,25},{9,... | collective-permute-start | bytes 491528 | tf_op jit(solution)/shard_map/ppermute | solution.py:43
  159.3 9.8 %collective-permute-start.23 = (bf16[512,256]{1,0:T(8,128)(2,1)S(1)}, bf16[512,256]{1,0:T(8,128)(2,1)S(1)}, u32[]{:S(2)}, u32[]{:S(2)}) collective-permute-start(bf16[512,256]{1,0:T(8,128)(2,1)S(1)} %get-tuple-element.101), channel_id=1, source_target_pairs={{0,16},{1,17},{2,18},{3,19},{4,20},{5,21},{6,22},{7,23},{8,24},{9,... | collective-permute-start | bytes 786440 | tf_op jit(solution)/shard_map/ppermute | solution.py:43
  160.9 9.3 %collective-permute-start.24 = (bf16[512,256]{1,0:T(8,128)(2,1)S(1)}, bf16[512,256]{1,0:T(8,128)(2,1)S(1)}, u32[]{:S(2)}, u32[]{:S(2)}) collective-permute-start(bf16[512,256]{1,0:T(8,128)(2,1)S(1)} %get-tuple-element.100), channel_id=1, source_target_pairs={{0,1},{1,0},{2,3},{3,2},{4,5},{5,4},{6,7},{7,6},{8,9},{9,8},{10,11... | collective-permute-start | bytes 786440 | tf_op jit(solution)/shard_map/ppermute | solution.py:43
  170.3 17.3 %collective-permute-start.33 = (bf16[40,512]{1,0:T(8,128)(2,1)S(1)}, bf16[40,512]{1,0:T(8,128)(2,1)S(1)}, u32[]{:S(2)}, u32[]{:S(2)}) collective-permute-start(bf16[40,512]{1,0:T(8,128)(2,1)S(1)} %get-tuple-element.117), channel_id=1, source_target_pairs={{0,2},{1,3},{2,0},{3,1},{4,6},{5,7},{6,4},{7,5},{8,10},{9,11},{10,... | collective-permute-start | bytes 122888 | tf_op jit(solution)/shard_map/ppermute | solution.py:43
  170.5 17.1 %collective-permute-start.34 = (bf16[40,512]{1,0:T(8,128)(2,1)S(1)}, bf16[40,512]{1,0:T(8,128)(2,1)S(1)}, u32[]{:S(2)}, u32[]{:S(2)}) collective-permute-start(bf16[40,512]{1,0:T(8,128)(2,1)S(1)} %get-tuple-element.119), channel_id=1, source_target_pairs={{0,4},{1,5},{2,6},{3,7},{4,0},{5,1},{6,2},{7,3},{8,12},{9,13},{10,... | collective-permute-start | bytes 122888 | tf_op jit(solution)/shard_map/ppermute | solution.py:43
  176.6 11.0 %collective-permute-start.35 = (bf16[40,512]{1,0:T(8,128)(2,1)S(1)}, bf16[40,512]{1,0:T(8,128)(2,1)S(1)}, u32[]{:S(2)}, u32[]{:S(2)}) collective-permute-start(bf16[40,512]{1,0:T(8,128)(2,1)S(1)} %get-tuple-element.118), channel_id=1, source_target_pairs={{0,6},{1,7},{2,4},{3,5},{4,2},{5,3},{6,0},{7,1},{8,14},{9,15},{10,... | collective-permute-start | bytes 122888 | tf_op jit(solution)/shard_map/ppermute | solution.py:43
  179.2 8.5 %collective-permute-start.31 = (bf16[512,256]{1,0:T(8,128)(2,1)S(1)}, bf16[512,256]{1,0:T(8,128)(2,1)S(1)}, u32[]{:S(2)}, u32[]{:S(2)}) collective-permute-start(bf16[512,256]{1,0:T(8,128)(2,1)S(1)} %add_convert_fusion.2), channel_id=1, source_target_pairs={{0,2},{1,3},{2,0},{3,1},{4,6},{5,7},{6,4},{7,5},{8,10},{9,11},{10,... | collective-permute-start | bytes 786440 | tf_op jit(solution)/shard_map/ppermute | solution.py:43
  179.8 7.7 %collective-permute-start.32 = (f32[64,128]{1,0:T(8,128)S(1)}, f32[64,128]{1,0:T(8,128)S(1)}, u32[]{:S(2)}, u32[]{:S(2)}) collective-permute-start(f32[64,128]{1,0:T(8,128)S(1)} %add.212), channel_id=1, source_target_pairs={{0,2},{1,3},{2,0},{3,1},{4,6},{5,7},{6,4},{7,5},{8,10},{9,11},{10,... | collective-permute-start | bytes 98312 | tf_op jit(solution)/shard_map/ppermute | solution.py:43
  187.7 21.7 %copy-start.1 = (bf16[256,256]{1,0:T(8,128)(2,1)S(1)}, bf16[256,256]{1,0:T(8,128)(2,1)}, u32[]{:S(2)}) copy-start(bf16[256,256]{1,0:T(8,128)(2,1)} %param.13) | copy-start | bytes 393220
  187.7 11.1 %collective-permute-start.38 = (bf16[40,512]{1,0:T(8,128)(2,1)S(1)}, bf16[40,512]{1,0:T(8,128)(2,1)S(1)}, u32[]{:S(2)}, u32[]{:S(2)}) collective-permute-start(bf16[40,512]{1,0:T(8,128)(2,1)S(1)} %add_convert_fusion.6), channel_id=1, source_target_pairs={{0,6},{1,7},{2,4},{3,5},{4,2},{5,3},{6,0},{7,1},{8,14},{9,15},{10,... | collective-permute-start | bytes 122888 | tf_op jit(solution)/shard_map/ppermute | solution.py:43
  190.1 8.7 %collective-permute-start.39 = (bf16[40,512]{1,0:T(8,128)(2,1)S(1)}, bf16[40,512]{1,0:T(8,128)(2,1)S(1)}, u32[]{:S(2)}, u32[]{:S(2)}) collective-permute-start(bf16[40,512]{1,0:T(8,128)(2,1)S(1)} %add_convert_fusion.6), channel_id=1, source_target_pairs={{0,4},{1,5},{2,6},{3,7},{4,0},{5,1},{6,2},{7,3},{8,12},{9,13},{10,... | collective-permute-start | bytes 122888 | tf_op jit(solution)/shard_map/ppermute | solution.py:43
  190.1 8.7 %collective-permute-start.40 = (bf16[40,512]{1,0:T(8,128)(2,1)S(1)}, bf16[40,512]{1,0:T(8,128)(2,1)S(1)}, u32[]{:S(2)}, u32[]{:S(2)}) collective-permute-start(bf16[40,512]{1,0:T(8,128)(2,1)S(1)} %add_convert_fusion.6), channel_id=1, source_target_pairs={{0,2},{1,3},{2,0},{3,1},{4,6},{5,7},{6,4},{7,5},{8,10},{9,11},{10,... | collective-permute-start | bytes 122888 | tf_op jit(solution)/shard_map/ppermute | solution.py:43
  192.1 6.7 %collective-permute-start.37 = (f32[64,128]{1,0:T(8,128)S(1)}, f32[64,128]{1,0:T(8,128)S(1)}, u32[]{:S(2)}, u32[]{:S(2)}) collective-permute-start(f32[64,128]{1,0:T(8,128)S(1)} %add.228), channel_id=1, source_target_pairs={{0,4},{1,5},{2,6},{3,7},{4,0},{5,1},{6,2},{7,3},{8,12},{9,13},{10,... | collective-permute-start | bytes 98312 | tf_op jit(solution)/shard_map/ppermute | solution.py:43
  194.1 6.1 %collective-permute-start.36 = (bf16[256,256]{1,0:T(8,128)(2,1)S(1)}, bf16[256,256]{1,0:T(8,128)(2,1)S(1)}, u32[]{:S(2)}, u32[]{:S(2)}) collective-permute-start(bf16[256,256]{1,0:T(8,128)(2,1)S(1)} %add_convert_fusion.5), channel_id=1, source_target_pairs={{0,4},{1,5},{2,6},{3,7},{4,0},{5,1},{6,2},{7,3},{8,12},{9,13},{10,... | collective-permute-start | bytes 393224 | tf_op jit(solution)/shard_map/ppermute | solution.py:43
  200.2 7.3 %collective-permute-start.41 = (bf16[160,512]{1,0:T(8,128)(2,1)S(1)}, bf16[160,512]{1,0:T(8,128)(2,1)S(1)}, u32[]{:S(2)}, u32[]{:S(2)}) collective-permute-start(bf16[160,512]{1,0:T(8,128)(2,1)S(1)} %pad_maximum_fusion.4), channel_id=1, source_target_pairs={{0,17},{1,16},{2,19},{3,18},{4,21},{5,20},{6,23},{7,22},{8,25},{9,... | collective-permute-start | bytes 491528 | tf_op jit(solution)/shard_map/ppermute | solution.py:43
  201.9 7.2 %collective-permute-start.42 = (bf16[160,512]{1,0:T(8,128)(2,1)S(1)}, bf16[160,512]{1,0:T(8,128)(2,1)S(1)}, u32[]{:S(2)}, u32[]{:S(2)}) collective-permute-start(bf16[160,512]{1,0:T(8,128)(2,1)S(1)} %pad_maximum_fusion.4), channel_id=1, source_target_pairs={{0,1},{1,0},{2,3},{3,2},{4,5},{5,4},{6,7},{7,6},{8,9},{9,8},{10,11... | collective-permute-start | bytes 491528 | tf_op jit(solution)/shard_map/ppermute | solution.py:43
  201.9 7.2 %collective-permute-start.43 = (bf16[160,512]{1,0:T(8,128)(2,1)S(1)}, bf16[160,512]{1,0:T(8,128)(2,1)S(1)}, u32[]{:S(2)}, u32[]{:S(2)}) collective-permute-start(bf16[160,512]{1,0:T(8,128)(2,1)S(1)} %pad_maximum_fusion.4), channel_id=1, source_target_pairs={{0,16},{1,17},{2,18},{3,19},{4,20},{5,21},{6,22},{7,23},{8,24},{9,... | collective-permute-start | bytes 491528 | tf_op jit(solution)/shard_map/ppermute | solution.py:43
  209.3 2.2 %collective-permute-start.44 = (bf16[640,512]{1,0:T(8,128)(2,1)S(1)}, bf16[640,512]{1,0:T(8,128)(2,1)S(1)}, u32[]{:S(2)}, u32[]{:S(2)}) collective-permute-start(bf16[640,512]{1,0:T(8,128)(2,1)S(1)} %pad_maximum_fusion.1), channel_id=1, source_target_pairs={{0,8},{1,9},{2,10},{3,11},{4,12},{5,13},{6,14},{7,15},{8,0},{9,1},... | collective-permute-start | bytes 1966088 | tf_op jit(solution)/shard_map/ppermute | solution.py:43
  (1 other events, 0.7 us)
